TPU v7x, 32 devices: a whole 2x2x4 slice. The times are simulated.
32 devices in a mesh: mod: 8 (over z, y), dp: 4 (over x, core).
Axes of the slice: x: 2, y: 2, z: 4, core: 2. Of those that a mesh axis runs over, the one named last changes fastest.
Arguments:
- token_ids: int32 [2, 192, 32], P(None, 'mod'), may hold values from 0 to 31999
- targets: int32 [2, 192, 4], P(None, 'mod'), may hold values from 0 to 31999
- positions: int32 [2, 192, 4], P(None, 'mod'), may hold values from 0 to 31, as said below
- loss_mask: int32 [2, 192, 4], P(None, 'mod'), may hold values 0 or 1
- paths: int32 [2, 192], P(None, 'mod'), may hold values from 0 to 7, as said below
- attend: float32 [8, 896, 2688], P('mod', 'dp'), may hold values from -0.1875 to 0.1875
- output: float32 [8, 896, 896], P('mod', 'dp'), may hold values from -0.0625 to 0.0625
- widen: float32 [8, 896, 3584], P('mod', 'dp'), may hold values from -0.1875 to 0.1875
- narrow: float32 [8, 3584, 896], P('mod', 'dp'), may hold values from -0.009765625 to 0.009765625
- gains: float32 [8, 1792], P('mod', 'dp'), may hold values from 0.5 to 1.5
- table: float32 [32000, 896], P(('mod', 'dp')), may hold values from -0.2338536 to 0.2338536
- final_gain: float32 [896], P('mod'), may hold values from 0.5 to 1.5
- first_attend: float32 [8, 896, 2688], P('mod', 'dp'), may hold values from -7.6293945e-05 to 7.6293945e-05
- first_output: float32 [8, 896, 896], P('mod', 'dp'), may hold values from -7.6293945e-05 to 7.6293945e-05
- first_widen: float32 [8, 896, 3584], P('mod', 'dp'), may hold values from -2.3841858e-06 to 2.3841858e-06
- first_narrow: float32 [8, 3584, 896], P('mod', 'dp'), may hold values from -7.6293945e-05 to 7.6293945e-05
- first_gains: float32 [8, 1792], P('mod', 'dp'), may hold values from -7.6293945e-05 to 7.6293945e-05
- first_table: float32 [32000, 896], P(('mod', 'dp')), may hold values from -7.6293945e-05 to 7.6293945e-05
- first_final: float32 [896], P('mod'), may hold values from -7.6293945e-05 to 7.6293945e-05
- second_attend: float32 [8, 896, 2688], P('mod', 'dp'), may hold values from 2.3638971e-11 to 9.4555884e-11
- second_output: float32 [8, 896, 896], P('mod', 'dp'), may hold values from 2.3638971e-11 to 9.4555884e-11
- second_widen: float32 [8, 896, 3584], P('mod', 'dp'), may hold values from 6.08535e-14 to 2.4523054e-13
- second_narrow: float32 [8, 3584, 896], P('mod', 'dp'), may hold values from 2.3638971e-11 to 9.4555884e-11
- second_gains: float32 [8, 1792], P('mod', 'dp'), may hold values from 2.3638971e-11 to 9.4555884e-11
- second_table: float32 [32000, 896], P(('mod', 'dp')), may hold values from 2.3638971e-11 to 9.4555884e-11
- second_final: float32 [896], P('mod'), may hold values from 2.3638971e-11 to 9.4555884e-11
Outputs:
- loss: float32 [], replicated
- gradient_norm: float32 [], replicated
- new_attend: float32 [8, 896, 2688], P('mod', 'dp')
- new_output: float32 [8, 896, 896], P('mod', 'dp')
- new_widen: float32 [8, 896, 3584], P('mod', 'dp')
- new_narrow: float32 [8, 3584, 896], P('mod', 'dp')
- new_gains: float32 [8, 1792], P('mod', 'dp')
- new_table: float32 [32000, 896], P(('mod', 'dp'))
- new_final: float32 [896], P('mod')
- mean_attend: float32 [8, 896, 2688], P('mod', 'dp')
- mean_output: float32 [8, 896, 896], P('mod', 'dp')
- mean_widen: float32 [8, 896, 3584], P('mod', 'dp')
- mean_narrow: float32 [8, 3584, 896], P('mod', 'dp')
- mean_gains: float32 [8, 1792], P('mod', 'dp')
- mean_table: float32 [32000, 896], P(('mod', 'dp'))
- mean_final: float32 [896], P('mod')
- square_attend: float32 [8, 896, 2688], P('mod', 'dp')
- square_output: float32 [8, 896, 896], P('mod', 'dp')
- square_widen: float32 [8, 896, 3584], P('mod', 'dp')
- square_narrow: float32 [8, 3584, 896], P('mod', 'dp')
- square_gains: float32 [8, 1792], P('mod', 'dp')
- square_table: float32 [32000, 896], P(('mod', 'dp'))
- square_final: float32 [896], P('mod')
Inputs may be any that keep to these rules, and one draw needn't show every extreme that they name: Within one sequence the 4 positions differ. `paths`: the 6 sequences of one device (aligned blocks of rows of a micro-batch) name 6 different modules.
All inputs are finite; a program needn't handle non-finite values. No bound on the sum of `loss_mask` on one device may be relied on, other than what follows from the above.
Results may differ from a plain program's by a relative error of at most 0.0095.
Values may be sent and summed in bfloat16 or wider, within the bound.
A program may use at most 384 MiB of HBM per device.

v0:
```python
import jax
import jax.numpy as jnp
from jax import lax
from jax.sharding import PartitionSpec as P

HEAD_DIM = 64


NORM_EPS = 1e-05
CLIP_LIMIT = 0.05
BETA_ONE = 0.5
BETA_TWO = 0.5
ADAM_STEP = 10.0
ADAM_EPS = 1e-08
RATE_MATRIX = 0.03
RATE_GAIN = 0.3
DECAY_MATRIX = 0.1


def joined(value, axis, join):
    pieces = jax.tree.map(lambda part: lax.all_gather(part, axis), value)
    head = jax.tree.map(lambda part: part[0], pieces)
    tail = jax.tree.map(lambda part: part[1:], pieces)
    total, _ = lax.scan(lambda total, piece: (join(total, piece), None), head, tail)
    return total


def rms_scale(values, gain):
    return values * lax.rsqrt(jnp.mean(values * values, axis=-1, keepdims=True) + NORM_EPS) * gain


def rotate(values):
    length = values.shape[-3]
    half = values.shape[-1] // 2
    inverse = 10000.0 ** (-jnp.arange(half, dtype=jnp.float32) / half)
    angle = jnp.arange(length, dtype=jnp.float32)[:, None] * inverse[None, :]
    cosine = jnp.cos(angle)[:, None, :]
    sine = jnp.sin(angle)[:, None, :]
    first, second = (values[..., :half], values[..., half:])
    return jnp.concatenate(
        [first * cosine - second * sine, first * sine + second * cosine], axis=-1
    )


def left_product(left, right):
    return lax.dot_general(
        left, right, (((0,), (0,)), ((), ())), preferred_element_type=jnp.float32
    )


def right_product(left, right):
    return lax.dot_general(
        left, right, (((1,), (1,)), ((), ())), preferred_element_type=jnp.float32
    )


def attention_scores(queries, keys_in):
    length = queries.shape[1]
    scores = jnp.einsum("nqhe,nkhe->nhqk", queries, keys_in, preferred_element_type=jnp.float32)
    causal = jnp.arange(length)[:, None] >= jnp.arange(length)[None, :]
    return jnp.where(causal, scores * queries.shape[-1] ** (-0.5), -1e30)


def module_forward(weights, arrived):
    attend, output, widen, narrow, gains = weights
    count_in, length, width = arrived.shape
    layer_input = arrived.astype(jnp.float32).reshape(-1, width)
    normed_first = rms_scale(layer_input, gains[:width].astype(jnp.float32)).astype(jnp.bfloat16)
    mixed_heads = jnp.dot(normed_first, attend, preferred_element_type=jnp.float32)
    shape = (count_in, length, width // HEAD_DIM, HEAD_DIM)
    queries = rotate(mixed_heads[:, :width].reshape(shape)).astype(jnp.bfloat16)
    keys_in = rotate(mixed_heads[:, width : 2 * width].reshape(shape)).astype(jnp.bfloat16)
    values = mixed_heads[:, 2 * width :].reshape(shape).astype(jnp.bfloat16)
    scores = attention_scores(queries, keys_in)
    log_total = jax.scipy.special.logsumexp(scores, axis=-1)
    chances = jnp.exp(scores - log_total[..., None]).astype(jnp.bfloat16)
    head_outputs = jnp.einsum(
        "nhqk,nkhe->nqhe", chances, values, preferred_element_type=jnp.float32
    )
    head_outputs = head_outputs.reshape(-1, width).astype(jnp.bfloat16)
    middle_hidden = layer_input + jnp.dot(head_outputs, output, preferred_element_type=jnp.float32)
    normed_second = rms_scale(middle_hidden, gains[width:].astype(jnp.float32)).astype(jnp.bfloat16)
    upper_hidden = jnp.dot(normed_second, widen, preferred_element_type=jnp.float32)
    activation_output = jax.nn.gelu(upper_hidden, approximate=True).astype(jnp.bfloat16)
    result = middle_hidden + jnp.dot(activation_output, narrow, preferred_element_type=jnp.float32)
    saved = (
        layer_input,
        normed_first,
        queries,
        keys_in,
        values,
        log_total,
        head_outputs,
        middle_hidden,
        normed_second,
        upper_hidden,
        activation_output,
    )
    return (result.reshape(count_in, length, width).astype(jnp.bfloat16), saved)


def module_backward(weights, saved, arrived):
    attend, output, widen, narrow, gains = weights
    (
        layer_input,
        normed_first,
        queries,
        keys_in,
        values,
        log_total,
        head_outputs,
        middle_hidden,
        normed_second,
        upper_hidden,
        activation_output,
    ) = saved
    count_in, length, width = arrived.shape
    incoming = arrived.reshape(-1, width)
    grad_narrow = left_product(activation_output, incoming)
    grad_act = right_product(incoming, narrow)
    gelu_back = jax.vjp(lambda value: jax.nn.gelu(value, approximate=True), upper_hidden)[1]
    grad_upper = gelu_back(grad_act)[0].astype(jnp.bfloat16)
    grad_widen = left_product(normed_second, grad_upper)
    grad_normed_two = right_product(grad_upper, widen)
    norm_back = jax.vjp(rms_scale, middle_hidden, gains[width:].astype(jnp.float32))[1]
    grad_middle, grad_gain_two = norm_back(grad_normed_two)
    grad_middle = grad_middle + incoming.astype(jnp.float32)
    branch_grad = grad_middle.astype(jnp.bfloat16)
    grad_output = left_product(head_outputs, branch_grad)
    grad_heads = right_product(branch_grad, output).astype(jnp.bfloat16).reshape(queries.shape)
    scores = attention_scores(queries, keys_in)
    chances = jnp.exp(scores - log_total[..., None])
    grad_values = jnp.einsum(
        "nhqk,nqhe->nkhe",
        chances.astype(jnp.bfloat16),
        grad_heads,
        preferred_element_type=jnp.float32,
    )
    grad_chances = jnp.einsum(
        "nqhe,nkhe->nhqk", grad_heads, values, preferred_element_type=jnp.float32
    )
    delta = jnp.sum(chances * grad_chances, axis=-1, keepdims=True)
    grad_raw = (chances * (grad_chances - delta) * queries.shape[-1] ** (-0.5)).astype(jnp.bfloat16)
    grad_queries = jnp.einsum(
        "nhqk,nkhe->nqhe", grad_raw, keys_in, preferred_element_type=jnp.float32
    )
    grad_keys = jnp.einsum("nhqk,nqhe->nkhe", grad_raw, queries, preferred_element_type=jnp.float32)
    rotate_back = jax.vjp(rotate, jnp.zeros(queries.shape, jnp.float32))[1]
    grad_mixed = jnp.concatenate(
        [
            rotate_back(grad_queries)[0].reshape(-1, width),
            rotate_back(grad_keys)[0].reshape(-1, width),
            grad_values.reshape(-1, width),
        ],
        axis=1,
    ).astype(jnp.bfloat16)
    grad_attend = left_product(normed_first, grad_mixed)
    grad_normed = right_product(grad_mixed, attend)
    norm_back_one = jax.vjp(rms_scale, layer_input, gains[:width].astype(jnp.float32))[1]
    grad_inputs, grad_gain_one = norm_back_one(grad_normed)
    leaving = (grad_middle + grad_inputs).astype(jnp.bfloat16).reshape(count_in, length, width)
    grads = (
        grad_attend[None],
        grad_output[None],
        grad_widen[None],
        grad_narrow[None],
        jnp.concatenate([grad_gain_one, grad_gain_two])[None],
    )
    return (leaving, grads)


def reduce_weights(grads):
    return (
        lax.psum_scatter(grads[0], "dp", scatter_dimension=1, tiled=True),
        lax.psum_scatter(grads[1], "dp", scatter_dimension=1, tiled=True),
        lax.psum_scatter(grads[2], "dp", scatter_dimension=1, tiled=True),
        lax.psum_scatter(grads[3], "dp", scatter_dimension=1, tiled=True),
        lax.psum_scatter(grads[4], "dp", scatter_dimension=1, tiled=True),
    )


def combine_parts(earlier, later):
    top = jnp.maximum(earlier[0], later[0])
    return (
        top,
        earlier[1] * jnp.exp(earlier[0] - top) + later[1] * jnp.exp(later[0] - top),
        earlier[2] + later[2],
    )


def adam_step(weight, grad, first, second, rate, decay):
    mean = BETA_ONE * first + (1.0 - BETA_ONE) * grad
    square = BETA_TWO * second + (1.0 - BETA_TWO) * grad * grad
    mean_hat = mean / (1.0 - BETA_ONE**ADAM_STEP)
    square_hat = square / (1.0 - BETA_TWO**ADAM_STEP)
    return (
        weight - rate * (mean_hat / (jnp.sqrt(square_hat) + ADAM_EPS) + decay * weight),
        mean,
        square,
    )


def on_device(
    token_ids,
    targets,
    positions,
    loss_mask,
    paths,
    attend,
    output,
    widen,
    narrow,
    gains,
    table,
    final_gain,
    first_attend,
    first_output,
    first_widen,
    first_narrow,
    first_gains,
    first_table,
    first_final,
    second_attend,
    second_output,
    second_widen,
    second_narrow,
    second_gains,
    second_table,
    second_final,
):
    group_dp = lax.axis_size("dp")
    group_mod = lax.axis_size("mod")
    dp_place = lax.axis_index("dp")
    gathered = (
        lax.all_gather(attend.astype(jnp.bfloat16), "dp", axis=1, tiled=True),
        lax.all_gather(output.astype(jnp.bfloat16), "dp", axis=1, tiled=True),
        lax.all_gather(widen.astype(jnp.bfloat16), "dp", axis=1, tiled=True),
        lax.all_gather(narrow.astype(jnp.bfloat16), "dp", axis=1, tiled=True),
        lax.all_gather(gains.astype(jnp.bfloat16), "dp", axis=1, tiled=True),
    )
    weights = tuple((piece[0] for piece in gathered))
    table_local, gain_whole = (
        lax.all_gather(table.astype(jnp.bfloat16), "mod", axis=0, tiled=True),
        lax.all_gather(final_gain.astype(jnp.bfloat16), "mod", axis=0, tiled=True),
    )
    width = table.shape[1]
    shard_rows = table.shape[0]
    seq_dev = paths.shape[1] // group_dp
    length = token_ids.shape[2]
    vocab_local = table_local.shape[0]
    vocab_rows = jnp.arange(vocab_local)

    def locate(ident):
        owned = ident // shard_rows % group_dp == dp_place
        place = jnp.where(
            owned, ident // shard_rows // group_dp * shard_rows + ident % shard_rows, 0
        )
        return (owned, place)

    table_acc = jnp.zeros((vocab_local, width), jnp.float32)
    final_acc = jnp.zeros((width,), jnp.float32)
    loss_acc = jnp.float32(0.0)
    count_acc = jnp.float32(0.0)
    module_acc = None
    for batch in range(token_ids.shape[0]):
        idents = token_ids[batch]
        owned, place = locate(idents)
        pieces = jnp.take(table_local, place, axis=0) * owned[..., None].astype(jnp.bfloat16)
        token_embedding = lax.psum_scatter(
            pieces.astype(jnp.float32).astype(jnp.bfloat16), "dp", scatter_dimension=0, tiled=True
        )
        own_paths = lax.dynamic_slice_in_dim(paths[batch], dp_place * seq_dev, seq_dev)
        route_index = (own_paths[None, :] == jnp.arange(group_mod)[:, None]).astype(jnp.bfloat16)
        sending = jnp.einsum(
            "vq,qpt->vpt", route_index, token_embedding, preferred_element_type=jnp.float32
        ).astype(jnp.bfloat16)
        arrived = lax.all_to_all(sending, "mod", split_axis=0, concat_axis=0, tiled=True)
        result, saved = module_forward(weights, arrived)
        backward_pass = lax.all_to_all(result, "mod", split_axis=0, concat_axis=0, tiled=True)
        returned_rows = jnp.einsum(
            "hq,hfg->qfg", route_index, backward_pass, preferred_element_type=jnp.float32
        )
        spots = lax.dynamic_slice_in_dim(positions[batch], dp_place * seq_dev, seq_dev)
        final, final_back = jax.vjp(rms_scale, returned_rows, gain_whole.astype(jnp.float32))
        picked = jnp.take_along_axis(final, spots[:, :, None], axis=1).astype(jnp.bfloat16)
        scored = lax.all_gather(picked, "dp", axis=0, tiled=True).reshape(-1, width)
        logits = right_product(scored, table_local)
        wanted = targets[batch].reshape(-1)
        counted = loss_mask[batch].reshape(-1).astype(jnp.float32)
        target_owned, target_place = locate(wanted)
        chosen = jnp.take_along_axis(logits, target_place[:, None], axis=1)[
            :, 0
        ] * target_owned.astype(jnp.float32)
        local_top = jnp.max(logits, axis=1)
        local_total = jnp.sum(jnp.exp(logits - local_top[:, None]), axis=1)
        top, total, target_logit = joined((local_top, local_total, chosen), "dp", combine_parts)
        log_total = top + jnp.log(total)
        loss_acc = loss_acc + jnp.sum(counted * (log_total - target_logit))
        count_acc = count_acc + jnp.sum(counted)
        hits = ((vocab_rows[None, :] == target_place[:, None]) & target_owned[:, None]).astype(
            jnp.float32
        )
        grad_logits = (counted[:, None] * (jnp.exp(logits - log_total[:, None]) - hits)).astype(
            jnp.bfloat16
        )
        table_acc = table_acc + left_product(grad_logits, scored)
        grad_scored = jnp.dot(grad_logits, table_local, preferred_element_type=jnp.float32).reshape(
            -1, spots.shape[1], width
        )
        grad_picked = lax.psum_scatter(grad_scored, "dp", scatter_dimension=0, tiled=True)
        grad_final = (
            jnp.zeros((seq_dev, length, width), jnp.float32)
            .at[jnp.arange(seq_dev)[:, None], spots]
            .add(grad_picked)
        )
        grad_returned, grad_gain = final_back(grad_final)
        grad_sending = jnp.einsum(
            "vq,qpt->vpt",
            route_index,
            grad_returned.astype(jnp.bfloat16),
            preferred_element_type=jnp.float32,
        ).astype(jnp.bfloat16)
        grad_arrived = lax.all_to_all(grad_sending, "mod", split_axis=0, concat_axis=0, tiled=True)
        leaving, grads = module_backward(weights, saved, grad_arrived)
        backward_gradient = lax.all_to_all(leaving, "mod", split_axis=0, concat_axis=0, tiled=True)
        grad_embedded = jnp.einsum(
            "hq,hfg->qfg", route_index, backward_gradient, preferred_element_type=jnp.float32
        )
        group_grads, gain_parts = (
            lax.all_gather(grad_embedded.astype(jnp.bfloat16), "dp", axis=0, tiled=True).astype(
                grad_embedded.dtype
            ),
            lax.all_gather(
                grad_gain[None, :].astype(jnp.bfloat16), "dp", axis=0, tiled=True
            ).astype(jnp.float32),
        )
        table_acc = table_acc.at[place.reshape(-1)].add(
            group_grads.reshape(-1, width) * owned.reshape(-1, 1).astype(jnp.float32)
        )
        final_acc = final_acc + jnp.sum(gain_parts, axis=0)
        module_acc = (
            grads if module_acc is None else tuple((a + b for a, b in zip(module_acc, grads)))
        )
    module_shards = reduce_weights(module_acc)
    table_shard, final_shard = (
        lax.psum_scatter(table_acc, "mod", scatter_dimension=0, tiled=True),
        lax.psum_scatter(final_acc, "mod", scatter_dimension=0, tiled=True),
    )
    squares = sum((jnp.sum(g * g) for g in module_shards)) + jnp.sum(table_shard * table_shard)
    squares = squares + jnp.sum(final_shard * final_shard) / group_dp
    sum_squares, loss_total, count_total = lax.psum(
        (squares, loss_acc / group_dp, count_acc / group_dp), ("mod", "dp")
    )
    gradient_norm = jnp.sqrt(sum_squares) / count_total
    factor = CLIP_LIMIT / jnp.maximum(gradient_norm, CLIP_LIMIT) / count_total
    params = (attend, output, widen, narrow, gains, table, final_gain)
    shards = tuple(module_shards) + (table_shard, final_shard)
    firsts = (
        first_attend,
        first_output,
        first_widen,
        first_narrow,
        first_gains,
        first_table,
        first_final,
    )
    seconds = (
        second_attend,
        second_output,
        second_widen,
        second_narrow,
        second_gains,
        second_table,
        second_final,
    )
    rates = (RATE_MATRIX, RATE_MATRIX, RATE_MATRIX, RATE_MATRIX, RATE_GAIN, RATE_MATRIX, RATE_GAIN)
    decays = (DECAY_MATRIX, DECAY_MATRIX, DECAY_MATRIX, DECAY_MATRIX, 0.0, DECAY_MATRIX, 0.0)
    updated = [
        adam_step(w, g * factor, f, s, r, d)
        for w, g, f, s, r, d in zip(params, shards, firsts, seconds, rates, decays)
    ]
    loss = loss_total / count_total
    return (
        loss,
        gradient_norm,
        updated[0][0],
        updated[1][0],
        updated[2][0],
        updated[3][0],
        updated[4][0],
        updated[5][0],
        updated[6][0],
        updated[0][1],
        updated[1][1],
        updated[2][1],
        updated[3][1],
        updated[4][1],
        updated[5][1],
        updated[6][1],
        updated[0][2],
        updated[1][2],
        updated[2][2],
        updated[3][2],
        updated[4][2],
        updated[5][2],
        updated[6][2],
    )


def solution(mesh):
    placed = (
        P(None, "mod", None),
        P(None, "mod", None),
        P(None, "mod", None),
        P(None, "mod", None),
        P(None, "mod"),
        P("mod", "dp", None),
        P("mod", "dp", None),
        P("mod", "dp", None),
        P("mod", "dp", None),
        P("mod", "dp"),
        P(("mod", "dp"), None),
        P("mod"),
        P("mod", "dp", None),
        P("mod", "dp", None),
        P("mod", "dp", None),
        P("mod", "dp", None),
        P("mod", "dp"),
        P(("mod", "dp"), None),
        P("mod"),
        P("mod", "dp", None),
        P("mod", "dp", None),
        P("mod", "dp", None),
        P("mod", "dp", None),
        P("mod", "dp"),
        P(("mod", "dp"), None),
        P("mod"),
    )
    return jax.shard_map(
        on_device,
        mesh=mesh,
        in_specs=placed,
        out_specs=(
            P(),
            P(),
            P("mod", "dp", None),
            P("mod", "dp", None),
            P("mod", "dp", None),
            P("mod", "dp", None),
            P("mod", "dp"),
            P(("mod", "dp"), None),
            P("mod"),
            P("mod", "dp", None),
            P("mod", "dp", None),
            P("mod", "dp", None),
            P("mod", "dp", None),
            P("mod", "dp"),
            P(("mod", "dp"), None),
            P("mod"),
            P("mod", "dp", None),
            P("mod", "dp", None),
            P("mod", "dp", None),
            P("mod", "dp", None),
            P("mod", "dp"),
            P(("mod", "dp"), None),
            P("mod"),
        ),
        check_vma=False,
    )
```

profile of v0, /device:TPU:0, one launch (start us, length us, event | category | flops | bytes accessed | tf_op | source)
XLA Modules:
  0.0 1872.8 jit_solution(8279231362287503039)
XLA Ops:
  12.2 198.8 %all-gather.18.cloned.1.call-done = bf16[8000,896]{1,0:T(8,128)(2,1)} async-done(((bf16[1000,896]{1,0:T(8,128)(2,1)}), bf16[8000,896]{1,0:T(8,128)(2,1)}) %all-gather.18.cloned.1.call-update) | async-done | bytes 14336016 | tf_op jit(solution)/shard_map/all_gather | solution.py:243
  211.1 10.4 gather_fusion.3
  223.0 10.7 gather_fusion
  252.3 5.7 all-reduce.8
  258.9 19.4 %all-reduce.9 = bf16[896]{0:T(1024)(128)(2,1)S(1)} all-reduce(bf16[896]{0:T(1024)(128)(2,1)S(1)} %dynamic-update-slice.1), channel_id=1, replica_groups=mesh['mod'=8,'dp'=4] {'mod'}, use_global_device_ids=true, to_apply=%add.9 | all-reduce | flops 896 | bytes 3584
  288.8 6.2 all-to-all-done.2
  300.3 8.2 all-to-all-done
  310.8 7.2 all-gather.20.cloned.1.call-done
  350.4 9.0 subtract_convert_fusion.1
  367.2 21.8 %all-gather.24.cloned.1.call-done = bf16[1,896,3584]{2,1,0:T(8,128)(2,1)} async-done(((bf16[1,224,3584]{2,1,0:T(8,128)(2,1)}), bf16[1,896,3584]{2,1,0:T(8,128)(2,1)}) %all-gather.24.cloned.1.call-update) | async-done | bytes 6422544 | tf_op jit(solution)/shard_map/all_gather | solution.py:237
  389.0 6.7 fusion.28
  395.7 42.5 %all-gather.26.cloned.1.call-done = bf16[1,3584,896]{2,1,0:T(8,128)(2,1)} async-done(((bf16[1,896,896]{2,1,0:T(8,128)(2,1)}), bf16[1,3584,896]{2,1,0:T(8,128)(2,1)}) %all-gather.26.cloned.1.call-update) | async-done | bytes 6422544 | tf_op jit(solution)/shard_map/all_gather | solution.py:238
  438.3 7.0 fusion.106
  445.3 5.9 all-to-all-start.3
  461.3 5.3 fusion.30
  471.7 6.0 all-to-all-start.1
  485.0 5.6 all-to-all-done.1
  493.8 5.5 all_gather.78
  501.3 5.7 all_gather.84
  507.8 9.3 fusion.322
  521.8 10.0 fusion.323
  539.3 6.9 all-reduce.19
  555.7 5.1 all-gather.6
  569.7 5.5 all-gather.7
  593.7 9.3 fusion.295
  606.7 8.4 fusion.296
  622.6 27.7 %all-reduce.23.cloned.1.call-done = (f32[24,4,896]{2,1,0:T(4,128)}, f32[24,4,896]{2,1,0:T(4,128)}) async-done(((f32[24,4,896]{2,1,0:T(4,128)}, f32[24,4,896]{2,1,0:T(4,128)}), (f32[24,4,896]{2,1,0:T(4,128)}, f32[24,4,896]{2,1,0:T(4,128)})) %all-reduce.23.cloned.1.call-update) | async-done | bytes 688144
  657.4 5.3 scatter_fusion
  663.6 5.3 scatter_fusion.1
  679.6 5.1 all-to-all-start.4
  697.1 5.7 all-to-all-start.5
  703.1 7.5 fusion.46
  711.8 5.8 fusion.26
  717.7 7.6 fusion.53
  725.4 6.4 multiply_reduce_fusion.6
  743.1 6.4 convolution_bitcast_fusion.3
  749.5 6.3 convolution_bitcast_fusion.1
  764.8 6.3 convolution_bitcast_fusion
  771.1 6.4 convolution_bitcast_fusion.2
  783.3 7.4 multiply_add_fusion.5
  835.3 4.6 fusion.34
  839.9 5.1 fusion.143
  846.8 17.1 all_to_all.40
  865.1 16.0 all_to_all.41
  891.9 4.7 add_bitcast_fusion.3
  900.6 5.2 add_bitcast_fusion.2
  910.5 6.5 add_bitcast_fusion.1
  917.1 4.7 fusion.293
  921.8 7.3 add_bitcast_fusion
  930.9 17.4 fusion.294
  948.3 18.3 convolution_add_fusion
  966.6 30.9 %scatter_custom_fusion.2 = f32[8000,896]{1,0:T(8,128)} fusion(f32[8000,896]{1,0:T(8,128)} %convolution_add_fusion, s32[768]{0:T(1024)S(1)} %fusion.236, bf16[768,896]{1,0:T(8,128)(2,1)} %bitcast.402, f32[768]{0:T(1024)S(1)} %fusion.229), kind=kCustom, calls=%fused_computation.109 | custom fusion | flops 2064384 | bytes 30052352 | tf_op jit(solution)/shard_map/scatter-add | solution.py:337
  997.6 30.1 %scatter_custom_fusion.3 = f32[8000,896]{1,0:T(8,128)} fusion(f32[8000,896]{1,0:T(8,128)} %scatter_custom_fusion.2, s32[768]{0:T(1024)S(1)} %fusion.237, bf16[768,896]{1,0:T(8,128)(2,1)} %bitcast.403, f32[768]{0:T(1024)S(1)} %fusion.228), kind=kCustom, calls=%fused_computation.107 | custom fusion | flops 2064384 | bytes 30052352 | tf_op jit(solution)/shard_map/scatter-add | solution.py:337
  1032.3 5.4 all-gather.8
  1037.7 5.5 all-gather.9
  1043.3 20.6 %all-reduce.17 = f32[896]{0:T(1024)S(1)} all-reduce(f32[896]{0:T(1024)S(1)} %add.848), channel_id=18, replica_groups=mesh['mod'=8,'dp'=4] {'mod'}, use_global_device_ids=true, to_apply=%region_60.64.clone | all-reduce | flops 896 | bytes 7168
  1074.1 83.0 %reduce-scatter.21.cloned.1.call-done = f32[1,224,3584]{2,1,0:T(8,128)} async-done(((f32[1,896,3584]{2,1,0:T(8,128)}), f32[1,224,3584]{2,1,0:T(8,128)}) %reduce-scatter.21.cloned.1.call-update) | async-done | bytes 3211280 | tf_op jit(solution)/shard_map/reduce_scatter | solution.py:176
  1161.1 99.9 %reduce-scatter.23.cloned.1.call-done = f32[1,896,896]{2,1,0:T(8,128)} async-done(((f32[1,3584,896]{2,1,0:T(8,128)}), f32[1,896,896]{2,1,0:T(8,128)}) %reduce-scatter.23.cloned.1.call-update) | async-done | bytes 3211280 | tf_op jit(solution)/shard_map/reduce_scatter | solution.py:177
  1265.8 513.4 %reduce-scatter.27.cloned.1.call-done = f32[1000,896]{1,0:T(8,128)} async-done(((f32[8000,896]{1,0:T(8,128)}), f32[1000,896]{1,0:T(8,128)}) %reduce-scatter.27.cloned.1.call-update) | async-done | bytes 3584016
  1783.5 42.3 %all-reduce.18 = (f32[]{:T(128)}, f32[]{:T(128)}, f32[]{:T(128)}) all-reduce(f32[]{:T(128)S(6)} %div.455, f32[]{:T(128)S(6)} %div.456, f32[]{:T(128)S(6)} %add.849), channel_id=1, replica_groups=mesh['mod'=8,'dp'=4] {'mod','dp'}, use_global_device_ids=true, to_apply=%region_22.26 | all-reduce | flops 3 | bytes 24 | tf_op jit(solution)/shard_map/psum | solution.py:351
  1830.5 7.9 multiply_subtract_fusion.3
  1841.8 5.4 multiply_subtract_fusion.2
  1849.8 5.4 multiply_subtract_fusion.1
  1858.3 5.5 multiply_subtract_fusion
  (656 shorter events, 334.1 us)
Async XLA Ops:
  7.2 203.8 %all-gather.18.cloned.1.call-start = ((), (), s32[]{:S(2)}) async-start(), calls=%async_computation.16 | async-start | bytes 16128000 | tf_op jit(solution)/shard_map/all_gather | solution.py:243
  10.7 269.1 %reduce-scatter.15.cloned.1.call-start = ((), (), s32[]{:S(2)}) async-start(), calls=%async_computation.22 | async-start | bytes 1720320 | tf_op jit(solution)/shard_map/reduce_scatter | solution.py:269
  11.4 199.7 %copy-start.89 = (pred[1,24,32]{2,1,0:T(8,128)(4,1)}, pred[1,24,32]{2,1,0:T(8,128)(4,1)S(1)}, u32[]{:S(2)}) copy-start(pred[1,24,32]{2,1,0:T(8,128)(4,1)S(1)} %get-tuple-element.267) | copy-start | bytes 2308
  222.9 63.7 %reduce-scatter.13.cloned.1.call-start = ((), (), s32[]{:S(2)}) async-start(), calls=%async_computation.17 | async-start | bytes 1720320 | tf_op jit(solution)/shard_map/reduce_scatter | solution.py:269
  235.1 83.0 %all-gather.20.cloned.1.call-start = ((), (), s32[]{:S(2)}) async-start(), calls=%async_computation.18 | async-start | bytes 6021120 | tf_op jit(solution)/shard_map/all_gather | solution.py:235
  238.1 126.7 %all-gather.22.cloned.1.call-start = ((), (), s32[]{:S(2)}) async-start(), calls=%async_computation.19 | async-start | bytes 2007040 | tf_op jit(solution)/shard_map/all_gather | solution.py:236
  240.1 148.9 %all-gather.24.cloned.1.call-start = ((), (), s32[]{:S(2)}) async-start(), calls=%async_computation.20 | async-start | bytes 8028160 | tf_op jit(solution)/shard_map/all_gather | solution.py:237
  241.6 16.4 copy-start.153
  241.6 196.7 %all-gather.26.cloned.1.call-start = ((), (), s32[]{:S(2)}) async-start(), calls=%async_computation.21 | async-start | bytes 8028160 | tf_op jit(solution)/shard_map/all_gather | solution.py:238
  248.3 51.2 %copy-start.136 = (s32[96]{0:T(128)}, s32[96]{0:T(128)S(1)}, u32[]{:S(2)}) copy-start(s32[96]{0:T(128)S(1)} %rem.418) | copy-start | bytes 1156
  248.4 51.1 %copy-start.138 = (s32[96]{0:T(128)}, s32[96]{0:T(128)S(1)}, u32[]{:S(2)}) copy-start(s32[96]{0:T(128)S(1)} %div.467) | copy-start | bytes 1156
  248.7 50.8 %copy-start.140 = (pred[96]{0:T(512)(128)(4,1)}, pred[96]{0:T(512)(128)(4,1)S(1)}, u32[]{:S(2)}) copy-start(pred[96]{0:T(512)(128)(4,1)S(1)} %ne.614) | copy-start | bytes 292
  250.0 45.0 %copy-start.100 = (s32[1,24,4]{1,2,0:T(4,128)}, s32[1,24,4]{1,2,0:T(4,128)S(1)}, u32[]{:S(2)}) copy-start(s32[1,24,4]{1,2,0:T(4,128)S(1)} %get-tuple-element.288) | copy-start | bytes 1156
  250.1 45.0 %copy-start.102 = (s32[1,24,4]{1,2,0:T(4,128)}, s32[1,24,4]{1,2,0:T(4,128)S(1)}, u32[]{:S(2)}) copy-start(s32[1,24,4]{1,2,0:T(4,128)S(1)} %get-tuple-element.289) | copy-start | bytes 1156
  252.3 42.7 %copy-start.134 = (s32[96,1]{0,1:T(1,128)}, s32[96,1]{0,1:T(1,128)S(1)}, u32[]{:S(2)}) copy-start(s32[96,1]{0,1:T(1,128)S(1)} %get-tuple-element.326) | copy-start | bytes 1156
  252.3 42.7 %copy-start.135 = (s32[96,1]{0,1:T(1,128)}, s32[96,1]{0,1:T(1,128)S(1)}, u32[]{:S(2)}) copy-start(s32[96,1]{0,1:T(1,128)S(1)} %get-tuple-element.327) | copy-start | bytes 1156
  278.3 212.9 %copy-start.83 = (f32[896]{0:T(1024)}, f32[896]{0:T(1024)S(1)}, u32[]{:S(2)}) copy-start(f32[896]{0:T(1024)S(1)} %convert_element_type.324) | copy-start | bytes 10756
  279.1 15.9 copy-start.123
  279.2 30.7 %copy-start.94 = (f32[896]{0:T(1024)}, f32[896]{0:T(1024)S(1)}, u32[]{:S(2)}) copy-start(f32[896]{0:T(1024)S(1)} %get-tuple-element.123) | copy-start | bytes 10756
  279.2 181.6 %copy-start.65 = (f32[896]{0:T(1024)}, f32[896]{0:T(1024)S(1)}, u32[]{:S(2)}) copy-start(f32[896]{0:T(1024)S(1)} %get-tuple-element.122) | copy-start | bytes 10756
  281.9 13.1 all-to-all-start.2
  285.5 14.0 copy-start.125
  295.0 13.4 all-to-all-start
  300.1 50.3 %copy-start.79 = (f32[32,32]{1,0:T(8,128)}, f32[32,32]{1,0:T(8,128)S(1)}, u32[]{:S(2)}) copy-start(f32[32,32]{1,0:T(8,128)S(1)} %get-tuple-element.306) | copy-start | bytes 12292
  300.1 50.3 %copy-start.81 = (f32[32,32]{1,0:T(8,128)}, f32[32,32]{1,0:T(8,128)S(1)}, u32[]{:S(2)}) copy-start(f32[32,32]{1,0:T(8,128)S(1)} %get-tuple-element.307) | copy-start | bytes 12292
  308.5 151.4 %copy-start.28 = (bf16[8,32,896]{2,1,0:T(8,128)(2,1)}, bf16[8,32,896]{2,1,0:T(8,128)(2,1)S(1)}, u32[]{:S(2)}) copy-start(bf16[8,32,896]{2,1,0:T(8,128)(2,1)S(1)} %all-to-all-done) | copy-start | bytes 1376260
  364.8 31.0 %copy-start.38 = (bf16[256,896]{1,0:T(8,128)(2,1)}, bf16[256,896]{1,0:T(8,128)(2,1)S(1)}, u32[]{:S(2)}) copy-start(bf16[256,896]{1,0:T(8,128)(2,1)S(1)} %convert_element_type.337) | copy-start | bytes 1376260
  367.2 28.6 %copy-start.117 = (f32[256]{0:T(256)}, f32[256]{0:T(256)S(1)}, u32[]{:S(2)}) copy-start(f32[256]{0:T(256)S(1)} %get-tuple-element.310) | copy-start | bytes 3076
  367.2 71.1 %copy-start.7 = (f32[256,896]{1,0:T(8,128)}, f32[256,896]{1,0:T(8,128)S(1)}, u32[]{:S(2)}) copy-start(f32[256,896]{1,0:T(8,128)S(1)} %get-tuple-element.311) | copy-start | bytes 2752516
  367.2 28.5 %copy-start.91 = (f32[256]{0:T(256)}, f32[256]{0:T(256)S(1)}, u32[]{:S(2)}) copy-start(f32[256]{0:T(256)S(1)} %fusion.258) | copy-start | bytes 3076
  445.3 26.4 %all-to-all-start.3 = ((bf16[8,32,896]{2,1,0:T(8,128)(2,1)}), bf16[8,32,896]{2,1,0:T(8,128)(2,1)}, u32[]{:S(2)}, u32[]{:S(2)}) async-start(bf16[8,32,896]{2,1,0:T(8,128)(2,1)} %bitcast.406), calls=%async_computation.5 | async-start | bytes 917504 | tf_op jit(solution)/shard_map/all_to_all | solution.py:279
  468.6 14.2 copy-start.137
  468.6 14.2 copy-start.139
  468.6 14.2 copy-start.141
  468.6 14.2 copy-start.149
  468.6 14.8 copy-start.124
  471.7 18.9 %copy-start.126 = (s32[6]{0:T(128)S(1)}, s32[6]{0:T(128)}, u32[]{:S(2)}) copy-start(s32[6]{0:T(128)} %copy-done.125) | copy-start | bytes 76
  471.7 18.9 %all-to-all-start.1 = ((bf16[8,32,896]{2,1,0:T(8,128)(2,1)}), bf16[8,32,896]{2,1,0:T(8,128)(2,1)S(1)}, u32[]{:S(2)}, u32[]{:S(2)}) async-start(bf16[8,32,896]{2,1,0:T(8,128)(2,1)} %bitcast.23), calls=%async_computation.2 | async-start | bytes 917504 | tf_op jit(solution)/shard_map/all_to_all | solution.py:279
  477.7 172.6 %all-reduce.23.cloned.1.call-start = ((), (), s32[]{:S(2)}) async-start(), calls=%async_computation.31 | async-start | bytes 1376256
  499.4 17.7 copy-start.56
  679.6 17.5 all-to-all-start.4
  697.1 20.5 %all-to-all-start.5 = ((bf16[8,32,896]{2,1,0:T(8,128)(2,1)}), bf16[8,32,896]{2,1,0:T(8,128)(2,1)}, u32[]{:S(2)}, u32[]{:S(2)}) async-start(bf16[8,32,896]{2,1,0:T(8,128)(2,1)} %copy.425), calls=%async_computation.7 | async-start | bytes 917504 | tf_op jit(solution)/shard_map/all_to_all | solution.py:323
  702.8 263.8 %all-gather.28.cloned.1.call-start = ((), (), s32[]{:S(2)}) async-start(), calls=%async_computation.27 | async-start | bytes 1720320 | tf_op jit(solution)/shard_map/all_gather | solution.py:330
  845.1 18.8 %copy-start.127 = (s32[6]{0:T(128)S(1)}, s32[6]{0:T(128)}, u32[]{:S(2)}) copy-start(s32[6]{0:T(128)} %copy-done.125) | copy-start | bytes 76
  864.3 24.0 %copy-start.37 = (bf16[256,896]{1,0:T(8,128)(2,1)S(1)}, bf16[256,896]{1,0:T(8,128)(2,1)}, u32[]{:S(2)}) copy-start(bf16[256,896]{1,0:T(8,128)(2,1)} %copy-done.36) | copy-start | bytes 1376260
  865.1 132.5 %all-gather.30.cloned.1.call-start = ((), (), s32[]{:S(2)}) async-start(), calls=%async_computation.28 | async-start | bytes 1720320 | tf_op jit(solution)/shard_map/all_gather | solution.py:330
  882.9 182.3 %reduce-scatter.25.cloned.1.call-start = ((), (), s32[]{:S(2)}) async-start(), calls=%async_computation.29 | async-start | bytes 1146880
  891.8 175.2 %reduce-scatter.19.cloned.1.call-start = ((), (), s32[]{:S(2)}) async-start(), calls=%async_computation.24 | async-start | bytes 4014080 | tf_op jit(solution)/shard_map/reduce_scatter | solution.py:175
  896.6 172.7 %reduce-scatter.17.cloned.1.call-start = ((), (), s32[]{:S(2)}) async-start(), calls=%async_computation.23 | async-start | bytes 12042240 | tf_op jit(solution)/shard_map/reduce_scatter | solution.py:174
  905.9 251.2 %reduce-scatter.21.cloned.1.call-start = ((), (), s32[]{:S(2)}) async-start(), calls=%async_computation.25 | async-start | bytes 16056320 | tf_op jit(solution)/shard_map/reduce_scatter | solution.py:176
  917.0 344.0 %reduce-scatter.23.cloned.1.call-start = ((), (), s32[]{:S(2)}) async-start(), calls=%async_computation.26 | async-start | bytes 16056320 | tf_op jit(solution)/shard_map/reduce_scatter | solution.py:177
  929.2 850.0 %reduce-scatter.27.cloned.1.call-start = ((), (), s32[]{:S(2)}) async-start(), calls=%async_computation.30 | async-start | bytes 32256000
  930.9 17.5 copy-start.58
  930.9 17.5 copy-start.99
  930.9 17.5 copy-start.109
  930.9 17.4 copy-start.110
  930.9 17.4 copy-start.114
  1264.3 564.8 %copy-start.133 = (f32[1,448]{1,0:T(1,128)S(1)}, f32[1,448]{1,0:T(1,128)}, u32[]{:S(2)}) copy-start(f32[1,448]{1,0:T(1,128)} %param.45) | copy-start | bytes 5380
  1264.3 564.8 %copy-start.150 = (f32[1,448]{1,0:T(1,128)S(1)}, f32[1,448]{1,0:T(1,128)}, u32[]{:S(2)}) copy-start(f32[1,448]{1,0:T(1,128)} %param.52) | copy-start | bytes 5380
  1264.3 564.8 %copy-start.151 = (f32[1,448]{1,0:T(1,128)S(1)}, f32[1,448]{1,0:T(1,128)}, u32[]{:S(2)}) copy-start(f32[1,448]{1,0:T(1,128)} %param.59) | copy-start | bytes 5380
  1264.3 565.4 %copy-start.154 = (f32[112]{0:T(128)S(1)}, f32[112]{0:T(128)}, u32[]{:S(2)}) copy-start(f32[112]{0:T(128)} %param.47) | copy-start | bytes 1348
  1264.3 565.4 %copy-start.155 = (f32[112]{0:T(128)S(1)}, f32[112]{0:T(128)}, u32[]{:S(2)}) copy-start(f32[112]{0:T(128)} %param.54) | copy-start | bytes 1348
  1264.4 565.4 %copy-start.156 = (f32[112]{0:T(128)S(1)}, f32[112]{0:T(128)}, u32[]{:S(2)}) copy-start(f32[112]{0:T(128)} %param.61) | copy-start | bytes 1348
  1264.4 566.1 %copy-start.30 = (f32[1,224,2688]{2,1,0:T(8,128)S(1)}, f32[1,224,2688]{2,1,0:T(8,128)}, u32[]{:S(2)}) copy-start(f32[1,224,2688]{2,1,0:T(8,128)} %param.41) | copy-start | bytes 7225348
  (117 other events, 556.2 us)
Sparse Core Ops, SparseCore 0:
  10.8 200.1 all-gather.17
  223.0 24.9 reduce-scatter.14
  251.2 26.7 reduce-scatter.12
  280.0 37.9 all-gather.19
  320.0 19.8 all-gather.21
  341.9 47.0 all-gather.23
  391.1 47.0 all-gather.25
  617.0 33.2 all-reduce.22
  865.2 17.0 all-gather.27
  884.3 18.5 all-gather.29
  906.0 23.9 reduce-scatter.24
  933.0 38.2 reduce-scatter.18
  973.9 79.2 reduce-scatter.16
  1055.7 101.3 reduce-scatter.20
  1159.6 101.3 reduce-scatter.22
  1264.5 514.7 reduce-scatter.26
where the time goes:
time: 1890 us; the launch traced here: 1870 us
  waiting for transfers between devices  1020 us (54%)
  matrix products  240 us (13%)
  local copies, waits for them, and re-layouts  198 us (10%)
  other arithmetic  195 us (10%)
  blocking collectives  161 us (9%)
  between operations  32.5 us (2%)
  starting transfers between devices  31.4 us (2%)
    unnamed x19, waiting for transfers between devices  541 us
    all_gather x1, waiting for transfers between devices, on_device(): lax.all_gather(table.astype(jnp.bfloat16), 'mod', axis=0, tiled=True)  199 us
    reduce_scatter x1, waiting for transfers between devices, reduce_weights(): lax.psum_scatter(grads[3], 'dp', scatter_dimension=1, tiled=True)  99.9 us
    reduce_scatter x1, waiting for transfers between devices, reduce_weights(): lax.psum_scatter(grads[2], 'dp', scatter_dimension=1, tiled=True)  83 us
    dot_general x10, matrix products, left_product(): lax.dot_general(left, right, (((0,), (0,)), ((), ())), preferred_element_...  74.6 us
    dot_general x10, matrix products, right_product(): lax.dot_general(left, right, (((1,), (1,)), ((), ())), preferred_element_...  61.2 us
    scatter-add x2, other arithmetic, on_device(): table_acc.at[place.reshape(-1)]  61.1 us
    unnamed x4, blocking collectives  52.6 us
  transfers between devices with their start and end apart: 22, of which 12 were waited for; matrix products, arithmetic and copies ran while one was open for 16% of the time, Pallas kernels for 0%

commit v1 on v0

v1 whole, which is shorter than its diff:
```python
import jax
import jax.numpy as jnp
from jax import lax
from jax.sharding import PartitionSpec as P

HEAD_DIM = 64


NORM_EPS = 1e-05
CLIP_LIMIT = 0.05
BETA_ONE = 0.5
BETA_TWO = 0.5
ADAM_STEP = 10.0
ADAM_EPS = 1e-08
RATE_MATRIX = 0.03
RATE_GAIN = 0.3
DECAY_MATRIX = 0.1


def rms_scale(values, gain):
    return values * lax.rsqrt(jnp.mean(values * values, axis=-1, keepdims=True) + NORM_EPS) * gain


def rotary_tables(length):
    half = HEAD_DIM // 2
    inverse = 10000.0 ** (-jnp.arange(half, dtype=jnp.float32) / half)
    angle = jnp.arange(length, dtype=jnp.float32)[:, None] * inverse[None, :]
    return jnp.cos(angle), jnp.sin(angle)


def rotate(values, cosine, sine):
    half = values.shape[-1] // 2
    first, second = (values[..., :half], values[..., half:])
    return jnp.concatenate(
        [first * cosine - second * sine, first * sine + second * cosine], axis=-1
    )


def product(left, right):
    return jnp.dot(left, right, preferred_element_type=jnp.float32)


def left_product(left, right):
    return lax.dot_general(
        left, right, (((0,), (0,)), ((), ())), preferred_element_type=jnp.float32
    )


def right_product(left, right):
    return lax.dot_general(
        left, right, (((1,), (1,)), ((), ())), preferred_element_type=jnp.float32
    )


def adam_step(weight, grad, first, second, rate, decay):
    mean = BETA_ONE * first + (1.0 - BETA_ONE) * grad
    square = BETA_TWO * second + (1.0 - BETA_TWO) * grad * grad
    mean_hat = mean / (1.0 - BETA_ONE**ADAM_STEP)
    square_hat = square / (1.0 - BETA_TWO**ADAM_STEP)
    return (
        weight - rate * (mean_hat / (jnp.sqrt(square_hat) + ADAM_EPS) + decay * weight),
        mean,
        square,
    )


def one_hot(index, extent):
    return (index[..., None] == jnp.arange(extent, dtype=jnp.int32)).astype(jnp.bfloat16)


def distinct_ranks(shard, row, counted, shard_rows):
    key = jnp.where(counted, shard * shard_rows + row, -1)
    place = jnp.arange(key.shape[0], dtype=jnp.int32)
    repeated = jnp.any(
        (key[:, None] == key[None, :]) & (place[None, :] < place[:, None]), axis=1
    )
    leading = counted & ~repeated
    rank = jnp.sum(
        (
            leading[None, :]
            & (shard[None, :] == shard[:, None])
            & (key[None, :] < key[:, None])
        ).astype(jnp.int32),
        axis=1,
    )
    return leading, rank


def on_device(
    token_ids,
    targets,
    positions,
    loss_mask,
    paths,
    attend,
    output,
    widen,
    narrow,
    gains,
    table,
    final_gain,
    first_attend,
    first_output,
    first_widen,
    first_narrow,
    first_gains,
    first_table,
    first_final,
    second_attend,
    second_output,
    second_widen,
    second_narrow,
    second_gains,
    second_table,
    second_final,
):
    group_dp = lax.axis_size("dp")
    group_mod = lax.axis_size("mod")
    dp_place = lax.axis_index("dp")
    mod_place = lax.axis_index("mod")
    sources = group_mod * group_dp
    micro, per_mod, length = token_ids.shape
    spots_seq = positions.shape[2]
    seq_dev = per_mod // group_dp
    shard_rows, width = table.shape
    heads = width // HEAD_DIM
    slots = micro * sources
    slots_local = slots // group_dp
    low = jnp.bfloat16

    mixing = lax.all_gather(
        jnp.concatenate([attend[0], output[0]], axis=1).astype(low), "dp", axis=0, tiled=True
    )
    attend_low, output_low = mixing[:, : 3 * width], mixing[:, 3 * width :]
    widen_low = lax.all_to_all(
        widen[0].astype(low), "dp", split_axis=1, concat_axis=0, tiled=True
    )
    narrow_low = narrow[0].astype(low)
    table_low = table.astype(low)
    gain_rows = lax.all_gather(
        jnp.concatenate([gains[0], final_gain]).astype(low), ("mod", "dp"), axis=0, tiled=False
    ).reshape(group_mod, group_dp, -1)
    gain_part = gains.shape[1]
    own_gains = lax.dynamic_index_in_dim(gain_rows, mod_place, 0, keepdims=False)
    own_gains = own_gains[:, :gain_part].reshape(-1).astype(jnp.float32)
    gain_one, gain_two = own_gains[:width], own_gains[width:]
    gain_final = gain_rows[:, 0, gain_part:].reshape(-1).astype(jnp.float32)

    fields = jnp.concatenate(
        [token_ids, positions, targets, loss_mask, paths[..., None]], axis=-1
    )
    fields = lax.all_gather(fields, "mod", axis=1, tiled=True)
    fields = fields.reshape(micro, sources, seq_dev, -1)
    routes = fields[..., -1]
    own_match = routes == mod_place
    own = jnp.sum(jnp.where(own_match[..., None], fields[..., : length + spots_seq], 0), axis=2)
    own_tokens = own[..., :length].reshape(-1)
    own_spots = own[..., length:].reshape(slots, spots_seq)
    own_live = jnp.any(own_match, axis=2).reshape(slots)
    match = routes[None] == jnp.arange(group_mod, dtype=jnp.int32)[:, None, None, None]
    scoring = jnp.sum(
        jnp.where(match[..., None], fields[None, ..., length + spots_seq : -1], 0), axis=3
    )
    wanted = scoring[..., :spots_seq].reshape(-1)
    counted = scoring[..., spots_seq:].reshape(-1).astype(jnp.float32)
    count_total = jnp.sum(counted)

    owner = own_tokens // shard_rows
    row = own_tokens % shard_rows
    shard = owner // group_dp
    held = jnp.repeat(own_live, length) & (owner % group_dp == dp_place)
    leading, rank = distinct_ranks(shard, row, held, shard_rows)
    expected = -(-slots * seq_dev * length // (group_mod * sources))
    cap = min(-(-2 * expected // 16) * 16, -(-shard_rows // 16) * 16)
    rounds = lax.pmax(jnp.max(jnp.where(leading, rank // cap, 0)) + 1, ("mod", "dp"))

    def exchange_plan(turn):
        slot = rank - turn * cap
        inside = held & (slot >= 0) & (slot < cap)
        slot = jnp.where(inside, shard * cap + slot, -1)
        asked = jnp.sum(
            jnp.where(
                leading[None, :]
                & (slot[None, :] == jnp.arange(group_mod * cap, dtype=jnp.int32)[:, None]),
                row[None, :] + 1,
                0,
            ),
            axis=1,
        )
        asked = lax.all_to_all(
            asked.reshape(group_mod, cap), "mod", split_axis=0, concat_axis=0, tiled=True
        )
        return one_hot(slot, group_mod * cap), one_hot(asked.reshape(-1) - 1, shard_rows)

    def fetch(plan):
        spread, pick = plan
        sent = product(pick, table_low).astype(low).reshape(group_mod, cap, width)
        got = lax.all_to_all(sent, "mod", split_axis=0, concat_axis=0, tiled=True)
        return product(spread, got.reshape(-1, width)).astype(low)

    def give(plan, gradient):
        spread, pick = plan
        sent = left_product(spread, gradient).astype(low).reshape(group_mod, cap, width)
        got = lax.all_to_all(sent, "mod", split_axis=0, concat_axis=0, tiled=True)
        return left_product(pick, got.reshape(-1, width))

    plan = exchange_plan(0)
    rows = fetch(plan)
    rows = lax.while_loop(
        lambda state: state[0] < rounds,
        lambda state: (state[0] + 1, state[1] + fetch(exchange_plan(state[0]))),
        (jnp.int32(1), rows),
    )[1]
    inputs = lax.psum_scatter(rows, "dp", scatter_dimension=0, tiled=True)

    spots = lax.dynamic_slice_in_dim(own_spots, dp_place * slots_local, slots_local)
    cosine, sine = rotary_tables(length)
    here = spots[:, :, None] == jnp.arange(length, dtype=jnp.int32)
    chosen = here.astype(low)
    inputs_wide = inputs.astype(jnp.float32)
    normed_one = rms_scale(inputs_wide, gain_one).astype(low)
    mixed = product(normed_one, attend_low)
    shape = (slots_local, length, heads, HEAD_DIM)
    around = (cosine[:, None, :], sine[:, None, :])
    queries = rotate(mixed[:, :width].reshape(shape), *around).astype(low)
    queries = jnp.einsum(
        "skt,sthe->skhe", chosen, queries, preferred_element_type=jnp.float32
    ).astype(low)
    keys_in = rotate(mixed[:, width : 2 * width].reshape(shape), *around).astype(low)
    values = mixed[:, 2 * width :].reshape(shape).astype(low)
    scale = HEAD_DIM ** (-0.5)
    raw = jnp.einsum("skhe,sthe->shkt", queries, keys_in, preferred_element_type=jnp.float32)
    causal = jnp.arange(length, dtype=jnp.int32) <= spots[:, None, :, None]
    scores = jnp.where(causal, raw * scale, -1e30)
    log_weight = jax.scipy.special.logsumexp(scores, axis=-1)
    chances = jnp.exp(scores - log_weight[..., None])
    heads_out = jnp.einsum(
        "shkt,sthe->skhe", chances.astype(low), values, preferred_element_type=jnp.float32
    )
    heads_out = heads_out.reshape(-1, width).astype(low)
    picked_inputs = jnp.einsum(
        "skt,stw->skw",
        chosen,
        inputs.reshape(slots_local, length, width),
        preferred_element_type=jnp.float32,
    ).reshape(-1, width)
    middle = picked_inputs + product(heads_out, output_low)

    normed_two = rms_scale(middle, gain_two).astype(low)
    normed_all = lax.all_gather(normed_two, "dp", axis=0, tiled=True)
    upper = product(normed_all, widen_low)
    gelu = lambda value: jax.nn.gelu(value, approximate=True)
    activated = gelu(upper).astype(low)
    lifted = lax.psum_scatter(
        product(activated, narrow_low), "dp", scatter_dimension=0, tiled=True
    )
    returned = (middle + lifted).astype(low).astype(jnp.float32)

    final, final_back = jax.vjp(rms_scale, returned, gain_final)
    scored = lax.all_gather(final.astype(low), ("mod", "dp"), axis=0, tiled=True)
    logits = right_product(scored, table_low)
    target_row = wanted - (mod_place * group_dp + dp_place) * shard_rows
    hits = target_row[:, None] == jnp.arange(shard_rows, dtype=jnp.int32)
    local_top = jnp.max(logits, axis=1)
    local_total = jnp.sum(jnp.exp(logits - local_top[:, None]), axis=1)
    local_target = jnp.sum(jnp.where(hits, logits, 0.0), axis=1)
    stats = lax.all_gather(
        jnp.stack([local_top, local_total, local_target]), ("mod", "dp"), axis=0, tiled=False
    )
    top = jnp.max(stats[:, 0], axis=0)
    total = jnp.sum(stats[:, 1] * jnp.exp(stats[:, 0] - top), axis=0)
    log_total = top + jnp.log(total)
    loss_total = jnp.sum(counted * (log_total - jnp.sum(stats[:, 2], axis=0)))
    grad_logits = (
        counted[:, None] * (jnp.exp(logits - log_total[:, None]) - hits.astype(jnp.float32))
    ).astype(low)
    table_grad = left_product(grad_logits, scored)
    grad_picked = lax.psum_scatter(
        product(grad_logits, table_low), ("mod", "dp"), scatter_dimension=0, tiled=True
    )

    grad_returned, grad_final = final_back(grad_picked)
    incoming = grad_returned.astype(low)
    incoming_all = lax.all_gather(incoming, "dp", axis=0, tiled=True)
    grad_narrow = left_product(activated, incoming_all)
    grad_act = right_product(incoming_all, narrow_low)
    grad_upper = jax.vjp(gelu, upper)[1](grad_act)[0].astype(low)
    grad_widen = left_product(normed_all, grad_upper)
    grad_widen = lax.all_to_all(grad_widen, "dp", split_axis=0, concat_axis=1, tiled=True)
    grad_normed_two = lax.psum_scatter(
        right_product(grad_upper, widen_low), "dp", scatter_dimension=0, tiled=True
    )
    grad_middle, grad_gain_two = jax.vjp(rms_scale, middle, gain_two)[1](grad_normed_two)
    grad_middle = grad_middle + incoming.astype(jnp.float32)

    branch_grad = grad_middle.astype(low)
    grad_output = left_product(heads_out, branch_grad)
    grad_heads = right_product(branch_grad, output_low).astype(low).reshape(queries.shape)
    grad_values = jnp.einsum(
        "shkt,skhe->sthe", chances.astype(low), grad_heads, preferred_element_type=jnp.float32
    )
    grad_chances = jnp.einsum(
        "skhe,sthe->shkt", grad_heads, values, preferred_element_type=jnp.float32
    )
    delta = jnp.sum(chances * grad_chances, axis=-1, keepdims=True)
    grad_raw = (chances * (grad_chances - delta) * scale).astype(low)
    grad_queries = jnp.einsum(
        "shkt,sthe->skhe", grad_raw, keys_in, preferred_element_type=jnp.float32
    )
    grad_keys = jnp.einsum(
        "shkt,skhe->sthe", grad_raw, queries, preferred_element_type=jnp.float32
    )
    spot_cosine = jnp.sum(jnp.where(here[..., None], cosine, 0.0), axis=2)[:, :, None, :]
    spot_sine = jnp.sum(jnp.where(here[..., None], sine, 0.0), axis=2)[:, :, None, :]
    grad_queries = rotate(grad_queries, spot_cosine, -spot_sine).astype(low)
    grad_queries = jnp.einsum(
        "skt,skhe->sthe", chosen, grad_queries, preferred_element_type=jnp.float32
    )
    grad_keys = rotate(grad_keys, around[0], -around[1])
    grad_mixed = jnp.concatenate(
        [part.reshape(-1, width) for part in (grad_queries, grad_keys, grad_values)], axis=1
    ).astype(low)
    grad_attend = left_product(normed_one, grad_mixed)
    grad_normed = right_product(grad_mixed, attend_low)
    grad_inputs, grad_gain_one = jax.vjp(rms_scale, inputs_wide, gain_one)[1](grad_normed)
    grad_skip = jnp.sum(
        jnp.where(
            here[..., None], grad_middle.reshape(slots_local, spots_seq, 1, width), 0.0
        ),
        axis=1,
    ).reshape(-1, width)
    leaving = (grad_skip + grad_inputs).astype(low)
    leaving_all = lax.all_gather(leaving, "dp", axis=0, tiled=True)

    table_grad = table_grad + give(plan, leaving_all)
    table_grad = lax.while_loop(
        lambda state: state[0] < rounds,
        lambda state: (
            state[0] + 1,
            state[1] + give(exchange_plan(state[0]), leaving_all),
        ),
        (jnp.int32(1), table_grad),
    )[1]
    grad_mixing = lax.psum_scatter(
        jnp.concatenate([grad_attend, grad_output], axis=1), "dp", scatter_dimension=0, tiled=True
    )
    gain_grads = lax.all_gather(
        jnp.concatenate([grad_gain_one, grad_gain_two, grad_final]),
        ("mod", "dp"),
        axis=0,
        tiled=False,
    ).reshape(group_mod, group_dp, -1)
    grad_gains = jnp.sum(
        lax.dynamic_index_in_dim(gain_grads, mod_place, 0, keepdims=False), axis=0
    )
    grad_gains = lax.dynamic_slice_in_dim(grad_gains, dp_place * gain_part, gain_part)
    final_part = final_gain.shape[0]
    grad_final = lax.dynamic_slice_in_dim(
        jnp.sum(gain_grads[:, :, 2 * width :], axis=(0, 1)), mod_place * final_part, final_part
    )
    module_grads = (
        grad_mixing[None, :, : 3 * width],
        grad_mixing[None, :, 3 * width :],
        grad_widen[None],
        grad_narrow[None],
        grad_gains[None],
    )
    squares = sum((jnp.sum(g * g) for g in module_grads)) + jnp.sum(table_grad * table_grad)
    squares = squares + jnp.sum(grad_final * grad_final) / group_dp
    gradient_norm = jnp.sqrt(lax.psum(squares, ("mod", "dp"))) / count_total
    factor = CLIP_LIMIT / jnp.maximum(gradient_norm, CLIP_LIMIT) / count_total
    params = (attend, output, widen, narrow, gains, table, final_gain)
    grads = module_grads + (table_grad, grad_final)
    firsts = (
        first_attend,
        first_output,
        first_widen,
        first_narrow,
        first_gains,
        first_table,
        first_final,
    )
    seconds = (
        second_attend,
        second_output,
        second_widen,
        second_narrow,
        second_gains,
        second_table,
        second_final,
    )
    rates = (RATE_MATRIX, RATE_MATRIX, RATE_MATRIX, RATE_MATRIX, RATE_GAIN, RATE_MATRIX, RATE_GAIN)
    decays = (DECAY_MATRIX, DECAY_MATRIX, DECAY_MATRIX, DECAY_MATRIX, 0.0, DECAY_MATRIX, 0.0)
    updated = [
        adam_step(w, g * factor, f, s, r, c)
        for w, g, f, s, r, c in zip(params, grads, firsts, seconds, rates, decays)
    ]
    return (
        loss_total / count_total,
        gradient_norm,
        *(entry[0] for entry in updated),
        *(entry[1] for entry in updated),
        *(entry[2] for entry in updated),
    )


def solution(mesh):
    placed = (
        P(None, "mod", None),
        P(None, "mod", None),
        P(None, "mod", None),
        P(None, "mod", None),
        P(None, "mod"),
        P("mod", "dp", None),
        P("mod", "dp", None),
        P("mod", "dp", None),
        P("mod", "dp", None),
        P("mod", "dp"),
        P(("mod", "dp"), None),
        P("mod"),
        P("mod", "dp", None),
        P("mod", "dp", None),
        P("mod", "dp", None),
        P("mod", "dp", None),
        P("mod", "dp"),
        P(("mod", "dp"), None),
        P("mod"),
        P("mod", "dp", None),
        P("mod", "dp", None),
        P("mod", "dp", None),
        P("mod", "dp", None),
        P("mod", "dp"),
        P(("mod", "dp"), None),
        P("mod"),
    )
    return jax.shard_map(
        on_device,
        mesh=mesh,
        in_specs=placed,
        out_specs=(
            P(),
            P(),
            P("mod", "dp", None),
            P("mod", "dp", None),
            P("mod", "dp", None),
            P("mod", "dp", None),
            P("mod", "dp"),
            P(("mod", "dp"), None),
            P("mod"),
            P("mod", "dp", None),
            P("mod", "dp", None),
            P("mod", "dp", None),
            P("mod", "dp", None),
            P("mod", "dp"),
            P(("mod", "dp"), None),
            P("mod"),
            P("mod", "dp", None),
            P("mod", "dp", None),
            P("mod", "dp", None),
            P("mod", "dp", None),
            P("mod", "dp"),
            P(("mod", "dp"), None),
            P("mod"),
        ),
        check_vma=False,
    )
```

time: 1890 us -> 970 us (0.51)
  waiting for transfers between devices: 1020 us -> 325 us
  local copies, waits for them, and re-layouts: 198 us -> 70.8 us
  matrix products: 240 us -> 127 us
  blocking collectives: 161 us -> 266 us
  other arithmetic: 195 us -> 117 us
    unnamed x19 -> x8, waiting for transfers between devices: 541 us -> 0.13 us
    all_gather x6, blocking collectives: 32.7 us -> 184 us  [the longest x1 43.2 us: on_device(): lax.all_gather(jnp.concatenate([grad_gain_one, grad_gain_two, grad_final]...]
    all_gather x7 -> x3, waiting for transfers between devices: 270 us -> 119 us  [the longest x1 59.9 us: on_device(): lax.all_gather(final.astype(low), ('mod', 'dp'), axis=0, tiled=True)]
    scatter-add x4 -> x0, other arithmetic: 71.7 us -> none  [the longest x2 61.1 us: on_device(): table_acc.at[place.reshape(-1)]]
    unnamed x4 -> x0, blocking collectives: 52.6 us -> none
    pmax x0 -> x1, blocking collectives: none -> 43 us  [on_device(): lax.pmax(jnp.max(jnp.where(leading, rank // cap, 0)) + 1, ('mod', 'dp'))]
    dot_general x10 -> x7, matrix products: 74.6 us -> 33 us  [left_product(): lax.dot_general(left, right, (((0,), (0,)), ((), ())), preferred_element_...]
    dot_general x10 -> x5, matrix products: 61.2 us -> 22.9 us  [right_product(): lax.dot_general(left, right, (((1,), (1,)), ((), ())), preferred_element_...]
  transfers between devices with their start and end apart: 22 -> 13, of which waited for: 12 -> 8; matrix products, arithmetic and copies ran while one was open for 16% -> 8% of each run, Pallas kernels for 0% -> 0%
where the time goes in v1:
time: 970 us; the launch traced here: 958 us
  waiting for transfers between devices  325 us (34%)
  blocking collectives  266 us (27%)
  matrix products  127 us (13%)
  other arithmetic  117 us (12%)
  local copies, waits for them, and re-layouts  70.8 us (7%)
  between operations  26.4 us (3%)
  starting transfers between devices  23.4 us (2%)
    reduce_scatter x1, waiting for transfers between devices, on_device(): lax.psum_scatter(product(grad_logits, table_low), ('mod', 'dp'), scatter_...  145 us
    all_gather x1, waiting for transfers between devices, on_device(): lax.all_gather(final.astype(low), ('mod', 'dp'), axis=0, tiled=True)  59.9 us
    all_gather x1, blocking collectives, on_device(): lax.all_gather(jnp.concatenate([grad_gain_one, grad_gain_two, grad_final]...  43.2 us
    pmax x1, blocking collectives, on_device(): lax.pmax(jnp.max(jnp.where(leading, rank // cap, 0)) + 1, ('mod', 'dp'))  43 us
    all_gather x1, blocking collectives, on_device(): lax.all_gather(jnp.stack([local_top, local_total, local_target]), ('mod',...  42.3 us
    all_gather x1, blocking collectives, on_device(): lax.all_gather(jnp.concatenate([gains[0], final_gain]).astype(low), ('mod...  41.5 us
    psum x1, blocking collectives, on_device(): gradient_norm = jnp.sqrt(lax.psum(squares, ('mod', 'dp'))) / count_total  39 us
    all_gather x1, waiting for transfers between devices, on_device(): lax.all_gather(jnp.concatenate([attend[0], output[0]], axis=1).astype(low...  36.8 us
  transfers between devices with their start and end apart: 13, of which 8 were waited for; matrix products, arithmetic and copies ran while one was open for 8% of the time, Pallas kernels for 0%

profile of v1, /device:TPU:0, one launch (start us, length us, event | category | flops | bytes accessed | tf_op | source)
XLA Modules:
  0.0 958.4 jit_solution(12865985040055076390)
XLA Ops:
  11.1 32.4 %all_gather.34 = s32[2,192,45]{2,1,0:T(8,128)S(1)} all-gather(s32[2,24,45]{2,1,0:T(8,128)S(1)} %concatenate.46), channel_id=1, replica_groups=mesh['mod'=8,'dp'=4] {'mod'}, dimensions={1}, use_global_device_ids=true | all-gather | bytes 77760 | tf_op jit(solution)/shard_map/all_gather | solution.py:152
  45.9 5.1 fusion.15
  51.6 6.4 convert_reduce_fusion
  60.8 5.5 all-to-all-start.4
  66.4 3.4 convert_element_type.162
  69.8 3.0 all-to-all-done.4
  72.9 4.4 fusion.49
  77.3 3.6 all-to-all-start.5
  83.5 43.0 %pmax.7 = s32[]{:T(128)} all-reduce(s32[]{:T(128)S(6)} %add.473), channel_id=1, replica_groups=mesh['mod'=8,'dp'=4] {'mod','dp'}, use_global_device_ids=true, to_apply=%region_7.8 | all-reduce | flops 1 | bytes 8 | tf_op jit(solution)/shard_map/pmax | solution.py:175
  126.5 4.9 fusion.23
  135.9 41.5 %all-gather.2 = bf16[32,1,560]{2,1,0:T(2,128)(2,1)S(1)} all-gather(bf16[1,1,560]{2,1,0:T(2,128)(2,1)S(1)} %maximum_bitcast_fusion.1), channel_id=1, replica_groups=mesh['mod'=8,'dp'=4] {'mod','dp'}, dimensions={0}, use_global_device_ids=true | all-gather | bytes 36960 | tf_op jit(solution)/shard_map/all_gather | solution.py:140
  179.6 3.0 convert_element_type.176
  186.8 36.8 %all-gather.9.cloned.1.call-done = bf16[896,3584]{1,0:T(8,128)(2,1)} async-done(((bf16[224,3584]{1,0:T(8,128)(2,1)}), bf16[896,3584]{1,0:T(8,128)(2,1)}) %all-gather.9.cloned.1.call-update) | async-done | bytes 6422544 | tf_op jit(solution)/shard_map/all_gather | solution.py:131
  223.7 5.9 fusion.21
  231.1 4.3 reshape.777
  235.4 2.5 reshape.778
  237.9 8.5 fusion.174
  246.5 15.4 %subtract_convert_fusion.1 = (bf16[16,32,14,32]{3,1,2,0:T(8,128)(2,1)S(1)}, bf16[16,32,14,32]{3,1,2,0:T(8,128)(2,1)S(1)}, bf16[16,32,14,32]{3,1,2,0:T(8,128)(2,1)S(1)}, bf16[16,32,14,32]{3,1,2,0:T(8,128)(2,1)S(1)}) fusion(f32[16,32,14,32]{3,2,1,0:T(8,128)S(1)} %get-tuple-element.344, f32[16,32,14,32]{3,2,1,0:T(8,128)S(1)} %get-tuple-element.343, ...), kind=kLoop, calls=%fused_computation.58 | loop fusion | flops 3670016 | bytes 5513216 | tf_op jit(solution)/shard_map/convert.12
  265.2 2.4 convert_element_type.168
  267.6 3.7 all-to-all-start.6
  271.3 2.3 fusion.79
  277.0 18.4 %all_gather.37 = bf16[256,896]{1,0:T(8,128)(2,1)} all-gather(bf16[64,896]{1,0:T(8,128)(2,1)S(1)} %multiply_convert_fusion.2), channel_id=1, replica_groups=mesh['mod'=8,'dp'=4] {'dp'}, dimensions={0}, use_global_device_ids=true | all-gather | bytes 573440 | tf_op jit(solution)/shard_map/all_gather | solution.py:250
  298.0 3.6 fusion.53
  302.6 23.2 %reduce-scatter.8.cloned.1.call-done = f32[64,896]{1,0:T(8,128)} async-done(((f32[256,896]{1,0:T(8,128)}), f32[64,896]{1,0:T(8,128)}) %reduce-scatter.8.cloned.1.call-update) | async-done | bytes 229392 | tf_op jit(solution)/shard_map/reduce_scatter | solution.py:254
  329.7 59.9 %all-gather.11.cloned.1.call-done = bf16[2048,896]{1,0:T(8,128)(2,1)} async-done(((bf16[64,896]{1,0:T(8,128)(2,1)}), bf16[2048,896]{1,0:T(8,128)(2,1)}) %all-gather.11.cloned.1.call-update) | async-done | bytes 3670032 | tf_op jit(solution)/shard_map/all_gather | solution.py:260
  389.6 7.0 fusion.180
  396.6 2.4 exponential_reduce_fusion
  399.1 42.3 %all-gather.3 = f32[32,3,2048]{2,1,0:T(4,128)S(1)} all-gather(f32[1,3,2048]{2,1,0:T(4,128)S(1)} %maximum_bitcast_fusion), channel_id=2, replica_groups=mesh['mod'=8,'dp'=4] {'mod','dp'}, dimensions={0}, use_global_device_ids=true | all-gather | bytes 811008 | tf_op jit(solution)/shard_map/all_gather | solution.py:267
  442.8 8.4 fusion.161
  451.3 144.7 %reduce-scatter.10.cloned.1.call-done = f32[64,896]{1,0:T(8,128)} async-done(((f32[2048,896]{1,0:T(8,128)}), f32[64,896]{1,0:T(8,128)}) %reduce-scatter.10.cloned.1.call-update) | async-done | bytes 229392 | tf_op jit(solution)/shard_map/reduce_scatter | solution.py:278
  599.3 6.3 all_gather.41
  606.4 3.3 fusion.91
  614.6 17.8 %reduce-scatter.12.cloned.1.call-done = f32[64,896]{1,0:T(8,128)} async-done(((f32[256,896]{1,0:T(8,128)}), f32[64,896]{1,0:T(8,128)}) %reduce-scatter.12.cloned.1.call-update) | async-done | bytes 229392 | tf_op jit(solution)/shard_map/reduce_scatter | solution.py:290
  636.7 2.7 fusion.82
  641.2 3.7 convert_bitcast_fusion
  644.9 2.8 fusion.57
  647.7 14.1 %convolution_bitcast_fusion = f32[16,32,14,64]{3,1,2,0:T(8,128)} fusion(bf16[16,4,14,64]{3,1,2,0:T(4,128)(2,1)} %copy-done.34, f32[16,14,4,32]{3,2,1,0:T(4,128)} %fusion.57, f32[16,14,4,32]{3,2,1,0:T(4,128)S(1)} %get-tuple-element.380, f32[16,14,4]{2,1,0:T(8,128)} %copy-done.40), kind=kOutput, calls=%fused_computation.94 | convolution fusion | flops 3871647 | bytes 2182656 | tf_op jit(solution)/shard_map/shkt,skhe->sthe/dot_general | solution.py:310
  661.7 13.7 %convolution_bitcast_fusion.1 = f32[16,4,14,64]{3,1,2,0:T(4,128)} fusion(f32[16,14,4,32]{3,2,1,0:T(4,128)} %fusion.57, bf16[16,32,14,32]{3,1,2,0:T(8,128)(2,1)} %copy-done.14, bf16[16,32,14,32]{3,1,2,0:T(8,128)(2,1)S(1)} %copy-done.13, f32[16,14,4,32]{3,2,1,0:T(4,128)S(1)} %get-tuple-element.380, f32[16,14,4]{2,1,0:T(8,128)} %copy-done.40), kind=kOutput, calls=%fused_computation.130 | convolution fusion | flops 5706655 | bytes 1379840 | tf_op jit(solution)/shard_map/shkt,sthe->skhe/dot_general | solution.py:307
  676.2 2.3 copy.254
  678.5 2.3 reshape.782
  680.8 4.5 subtract_convert_fusion
  687.1 2.2 reshape.781
  692.3 2.2 reshape.780
  697.3 8.3 fusion.43
  710.3 3.0 fusion.105
  713.3 5.7 pad_maximum_fusion
  720.1 2.4 fusion.183
  722.5 3.8 all-to-all-start.7
  726.3 22.4 %all-gather.13.cloned.1.call-done = bf16[2048,896]{1,0:T(8,128)(2,1)} async-done(((bf16[512,896]{1,0:T(8,128)(2,1)}), bf16[2048,896]{1,0:T(8,128)(2,1)}) %all-gather.13.cloned.1.call-update) | async-done | bytes 3670032 | tf_op jit(solution)/shard_map/all_gather | solution.py:333
  748.7 6.7 fusion.50
  755.4 17.3 %all-to-all-done.7 = f32[4,224,896]{2,1,0:T(8,128)S(1)} async-done(((f32[4,224,896]{2,1,0:T(8,128)}), f32[4,224,896]{2,1,0:T(8,128)S(1)}, u32[]{:S(2)}, u32[]{:S(2)}) %all-to-all-start.7) | async-done | bytes 3211296 | tf_op jit(solution)/shard_map/all_to_all | solution.py:289
  772.7 5.8 all-to-all-start.8
  781.0 11.1 %fusion.160 = f32[1000,896]{1,0:T(8,128)} fusion(bf16[2048,896]{1,0:T(8,128)(2,1)} %all-gather.11.cloned.1.call-done, f32[2048,1000]{0,1:T(8,128)} %copy-done.10, f32[2048]{0:T(1024)} %copy-done.72, f32[2048]{0:T(1024)} %copy-done.71, s32[2048]{0:T(1024)S(1)} %copy-done.59), kind=kOutput, calls=%fused_computation.310 | convolution fusion | flops 3682304000 | bytes 15470592 | tf_op jit(solution)/shard_map/dot_general | solution.py:44
  792.1 3.1 multiply_reduce_fusion.1
  795.3 43.2 %all-gather.4 = f32[32,1,2688]{2,1,0:T(1,128)S(1)} all-gather(f32[1,1,2688]{2,1,0:T(1,128)S(1)} %reshape.795), channel_id=3, replica_groups=mesh['mod'=8,'dp'=4] {'mod','dp'}, dimensions={0}, use_global_device_ids=true | all-gather | bytes 354816 | tf_op jit(solution)/shard_map/all_gather | solution.py:347
  845.9 6.2 fusion.48
  853.2 3.7 multiply_reduce_fusion
  856.9 2.9 multiply_reduce_fusion.3
  867.0 39.0 %psum.7 = f32[]{:T(128)} all-reduce(f32[]{:T(128)S(6)} %add.499), channel_id=1, replica_groups=mesh['mod'=8,'dp'=4] {'mod','dp'}, use_global_device_ids=true, to_apply=%region_51.52 | all-reduce | flops 1 | bytes 8 | tf_op jit(solution)/shard_map/psum | solution.py:370
  911.2 2.5 mul.994
  915.0 9.9 %multiply_subtract_fusion = (f32[1000,896]{1,0:T(8,128)}, f32[1000,896]{1,0:T(8,128)}, f32[1000,896]{1,0:T(8,128)}) fusion(f32[1000,896]{1,0:T(8,128)} %param.40, f32[1000,896]{1,0:T(8,128)} %get-tuple-element.256, f32[]{:T(128)S(6)} %div.221, f32[1000,896]{1,0:T(8,128)} %param.47, f32[1000,896]{1,0:T(8,128)} %param.54), kind=kLoop, calls=%fused_computation.63 | loop fusion | flops 13440000 | bytes 25088004 | tf_op jit(solution)/shard_map/sub | solution.py:61
  927.6 5.4 multiply_subtract_fusion.1
  935.7 5.4 multiply_subtract_fusion.2
  944.8 4.4 multiply_subtract_fusion.3
  (339 shorter events, 94.1 us)
Async XLA Ops:
  43.7 26.1 %copy-start.30 = (s32[2,192,45]{2,0,1:T(2,128)}, s32[2,192,45]{2,0,1:T(2,128)S(1)}, u32[]{:S(2)}) copy-start(s32[2,192,45]{2,0,1:T(2,128)S(1)} %copy.221) | copy-start | bytes 207364
  58.8 67.7 %copy-start.69 = (s32[2048]{0:T(1024)}, s32[2048]{0:T(1024)S(1)}, u32[]{:S(2)}) copy-start(s32[2048]{0:T(1024)S(1)} %get-tuple-element.373) | copy-start | bytes 24580
  60.8 12.0 %all-to-all-start.4 = ((s32[8,1,96]{2,1,0:T(1,128)}), s32[8,1,96]{2,1,0:T(1,128)S(1)}, u32[]{:S(2)}, u32[]{:S(2)}) async-start(s32[8,1,96]{2,1,0:T(1,128)} %all_to_all.64), calls=%async_computation.4 | async-start | bytes 8192 | tf_op jit(solution)/shard_map/all_to_all | solution.py:190
  77.3 49.2 %all-to-all-start.5 = ((bf16[8,96,896]{2,1,0:T(8,128)(2,1)}), bf16[8,96,896]{2,1,0:T(8,128)(2,1)S(1)}, u32[]{:S(2)}, u32[]{:S(2)}) async-start(bf16[8,96,896]{2,1,0:T(8,128)(2,1)} %bitcast.8), calls=%async_computation.5 | async-start | bytes 2752512 | tf_op jit(solution)/shard_map/all_to_all | solution.py:198
  80.9 104.5 %reduce-scatter.6.cloned.1.call-start = ((), (), s32[]{:S(2)}) async-start(), calls=%async_computation.14 | async-start | bytes 4587520 | tf_op jit(solution)/shard_map/reduce_scatter | solution.py:214
  132.4 91.3 %all-gather.9.cloned.1.call-start = ((), (), s32[]{:S(2)}) async-start(), calls=%async_computation.15 | async-start | bytes 8028160 | tf_op jit(solution)/shard_map/all_gather | solution.py:131
  134.4 43.9 %copy-start.4 = (f32[1,224,3584]{2,1,0:T(8,128)S(1)}, f32[1,224,3584]{2,1,0:T(8,128)}, u32[]{:S(2)}) copy-start(f32[1,224,3584]{2,1,0:T(8,128)} %param.37) | copy-start | bytes 9633796
  177.8 45.8 %copy-start.65 = (f32[896]{0:T(1024)}, f32[896]{0:T(1024)S(1)}, u32[]{:S(2)}) copy-start(f32[896]{0:T(1024)S(1)} %slice.106) | copy-start | bytes 10756
  178.2 96.3 %copy-start.50 = (s32[16,4]{1,0:T(8,128)}, s32[16,4]{1,0:T(8,128)S(1)}, u32[]{:S(2)}) copy-start(s32[16,4]{1,0:T(8,128)S(1)} %copy.228) | copy-start | bytes 772
  178.3 98.7 %copy-start.54 = (f32[896]{0:T(1024)}, f32[896]{0:T(1024)S(1)}, u32[]{:S(2)}) copy-start(f32[896]{0:T(1024)S(1)} %slice.117) | copy-start | bytes 10756
  185.3 61.1 %copy-start.52 = (f32[32,32]{1,0:T(8,128)}, f32[32,32]{1,0:T(8,128)S(1)}, u32[]{:S(2)}) copy-start(f32[32,32]{1,0:T(8,128)S(1)} %get-tuple-element.377) | copy-start | bytes 12292
  186.8 42.8 %copy-start.61 = (f32[512]{0:T(512)}, f32[512]{0:T(512)S(1)}, u32[]{:S(2)}) copy-start(f32[512]{0:T(512)S(1)} %fusion.42) | copy-start | bytes 6148
  186.8 42.7 %copy-start.67 = (f32[512]{0:T(512)}, f32[512]{0:T(512)S(1)}, u32[]{:S(2)}) copy-start(f32[512]{0:T(512)S(1)} %fusion.145) | copy-start | bytes 6148
  265.2 8.4 copy-start.40
  267.6 6.9 copy-start.9
  267.6 27.8 %all-to-all-start.6 = ((bf16[224,4,896]{2,0,1:T(8,128)(2,1)}), bf16[224,4,896]{2,0,1:T(8,128)(2,1)S(1)}, u32[]{:S(2)}, u32[]{:S(2)}) async-start(bf16[224,4,896]{2,0,1:T(8,128)(2,1)} %copy.243), calls=%async_computation.7 | async-start | bytes 3211264 | tf_op jit(solution)/shard_map/all_to_all | solution.py:135
  271.3 54.6 %reduce-scatter.8.cloned.1.call-start = ((), (), s32[]{:S(2)}) async-start(), calls=%async_computation.16 | async-start | bytes 1146880 | tf_op jit(solution)/shard_map/reduce_scatter | solution.py:254
  276.9 24.8 %copy-start.84 = (f32[64]{0:T(128)}, f32[64]{0:T(128)S(1)}, u32[]{:S(2)}) copy-start(f32[64]{0:T(128)S(1)} %get-tuple-element.381) | copy-start | bytes 772
  276.9 49.0 %copy-start.15 = (f32[64,896]{1,0:T(8,128)}, f32[64,896]{1,0:T(8,128)S(1)}, u32[]{:S(2)}) copy-start(f32[64,896]{1,0:T(8,128)S(1)} %get-tuple-element.382) | copy-start | bytes 688132
  276.9 24.8 %copy-start.76 = (f32[64]{0:T(128)}, f32[64]{0:T(128)S(1)}, u32[]{:S(2)}) copy-start(f32[64]{0:T(128)S(1)} %fusion.149) | copy-start | bytes 772
  298.0 30.4 %copy-start.31 = (s32[2,192,45]{2,0,1:T(2,128)S(1)}, s32[2,192,45]{2,0,1:T(2,128)}, u32[]{:S(2)}) copy-start(s32[2,192,45]{2,0,1:T(2,128)} %copy-done.30) | copy-start | bytes 207364
  301.7 87.9 %all-gather.11.cloned.1.call-start = ((), (), s32[]{:S(2)}) async-start(), calls=%async_computation.17 | async-start | bytes 3784704 | tf_op jit(solution)/shard_map/all_gather | solution.py:260
  328.4 267.6 %reduce-scatter.10.cloned.1.call-start = ((), (), s32[]{:S(2)}) async-start(), calls=%async_computation.18 | async-start | bytes 7569408 | tf_op jit(solution)/shard_map/reduce_scatter | solution.py:278
  329.3 113.5 %copy-start.58 = (s32[2048]{0:T(1024)}, s32[2048]{0:T(1024)S(1)}, u32[]{:S(2)}) copy-start(s32[2048]{0:T(1024)S(1)} %sub.194) | copy-start | bytes 24580
  329.7 113.1 %copy-start.71 = (f32[2048]{0:T(1024)}, f32[2048]{0:T(1024)S(1)}, u32[]{:S(2)}) copy-start(f32[2048]{0:T(1024)S(1)} %convert_element_type.185) | copy-start | bytes 24580
  396.6 46.2 %copy-start.10 = (f32[2048,1000]{0,1:T(8,128)}, f32[2048,1000]{0,1:T(8,128)S(1)}, u32[]{:S(2)}) copy-start(f32[2048,1000]{0,1:T(8,128)S(1)} %get-tuple-element.384) | copy-start | bytes 24576004
  442.8 8.4 copy-start.72
  451.2 144.8 %copy-start.36 = (bf16[64,896]{1,0:T(8,128)(2,1)S(1)}, bf16[64,896]{1,0:T(8,128)(2,1)}, u32[]{:S(2)}) copy-start(bf16[64,896]{1,0:T(8,128)(2,1)} %copy-done.35) | copy-start | bytes 344068
  451.2 181.2 %reduce-scatter.12.cloned.1.call-start = ((), (), s32[]{:S(2)}) async-start(), calls=%async_computation.19 | async-start | bytes 1146880 | tf_op jit(solution)/shard_map/reduce_scatter | solution.py:290
  611.4 137.3 %all-gather.13.cloned.1.call-start = ((), (), s32[]{:S(2)}) async-start(), calls=%async_computation.21 | async-start | bytes 4587520 | tf_op jit(solution)/shard_map/all_gather | solution.py:333
  611.9 33.0 %copy-start.11 = (bf16[16,32,14,64]{3,2,1,0:T(8,128)(2,1)S(1)}, bf16[16,32,14,64]{3,2,1,0:T(8,128)(2,1)}, u32[]{:S(2)}) copy-start(bf16[16,32,14,64]{3,2,1,0:T(8,128)(2,1)} %convert_element_type.168) | copy-start | bytes 2752516
  647.7 14.1 %copy-start.13 = (bf16[16,32,14,32]{3,1,2,0:T(8,128)(2,1)S(1)}, bf16[16,32,14,32]{3,1,2,0:T(8,128)(2,1)}, u32[]{:S(2)}) copy-start(bf16[16,32,14,32]{3,1,2,0:T(8,128)(2,1)} %copy-done.12) | copy-start | bytes 1376260
  661.7 13.7 %copy-start.20 = (f32[64,896]{1,0:T(8,128)S(1)}, f32[64,896]{1,0:T(8,128)}, u32[]{:S(2)}) copy-start(f32[64,896]{1,0:T(8,128)} %copy-done.19) | copy-start | bytes 688132
  697.2 8.3 copy-start.48
  697.3 8.3 copy-start.62
  697.3 8.3 copy-start.43
  697.3 8.3 copy-start.53
  708.2 148.7 %reduce-scatter.14.cloned.1.call-start = ((), (), s32[]{:S(2)}) async-start(), calls=%async_computation.20 | async-start | bytes 16056320 | tf_op jit(solution)/shard_map/reduce_scatter | solution.py:344
  722.5 26.3 %copy-start.70 = (s32[2048]{0:T(1024)S(1)}, s32[2048]{0:T(1024)}, u32[]{:S(2)}) copy-start(s32[2048]{0:T(1024)} %copy-done.69) | copy-start | bytes 24580
  722.5 50.2 %all-to-all-start.7 = ((f32[4,224,896]{2,1,0:T(8,128)}), f32[4,224,896]{2,1,0:T(8,128)S(1)}, u32[]{:S(2)}, u32[]{:S(2)}) async-start(f32[4,224,896]{2,1,0:T(8,128)} %bitcast.157), calls=%async_computation.12 | async-start | bytes 6422528 | tf_op jit(solution)/shard_map/all_to_all | solution.py:289
  726.3 52.2 %copy-start.57 = (f32[2048]{0:T(1024)S(1)}, f32[2048]{0:T(1024)}, u32[]{:S(2)}) copy-start(f32[2048]{0:T(1024)} %get-tuple-element.328) | copy-start | bytes 24580
  755.4 25.6 %copy-start.59 = (s32[2048]{0:T(1024)S(1)}, s32[2048]{0:T(1024)}, u32[]{:S(2)}) copy-start(s32[2048]{0:T(1024)} %copy-done.58) | copy-start | bytes 24580
  772.7 71.8 %copy-start = (f32[4,224,896]{2,1,0:T(8,128)}, f32[4,224,896]{2,1,0:T(8,128)S(1)}, u32[]{:S(2)}) copy-start(f32[4,224,896]{2,1,0:T(8,128)S(1)} %all-to-all-done.7) | copy-start | bytes 9633796
  772.7 73.2 %all-to-all-start.8 = ((bf16[8,96,896]{2,1,0:T(8,128)(2,1)}), bf16[8,96,896]{2,1,0:T(8,128)(2,1)}, u32[]{:S(2)}, u32[]{:S(2)}) async-start(bf16[8,96,896]{2,1,0:T(8,128)(2,1)} %bitcast.162), calls=%async_computation.13 | async-start | bytes 2752512 | tf_op jit(solution)/shard_map/all_to_all | solution.py:204
  781.0 11.1 %copy-start.18 = (f32[256,896]{1,0:T(8,128)S(1)}, f32[256,896]{1,0:T(8,128)}, u32[]{:S(2)}) copy-start(f32[256,896]{1,0:T(8,128)} %copy-done.17) | copy-start | bytes 2752516
  781.0 11.1 %copy-start.47 = (bf16[256,896]{1,0:T(8,128)(2,1)S(1)}, bf16[256,896]{1,0:T(8,128)(2,1)}, u32[]{:S(2)}) copy-start(bf16[256,896]{1,0:T(8,128)(2,1)} %copy-done.46) | copy-start | bytes 1376260
  845.9 6.2 copy-start.81
  853.2 55.6 %copy-start.1 = (f32[4,224,896]{2,1,0:T(8,128)S(1)}, f32[4,224,896]{2,1,0:T(8,128)}, u32[]{:S(2)}) copy-start(f32[4,224,896]{2,1,0:T(8,128)} %copy-done) | copy-start | bytes 9633796
  915.0 9.9 %copy-start.2 = (f32[1,896,896]{2,1,0:T(8,128)S(1)}, f32[1,896,896]{2,1,0:T(8,128)}, u32[]{:S(2)}) copy-start(f32[1,896,896]{2,1,0:T(8,128)} %param.38) | copy-start | bytes 9633796
  915.0 10.4 %copy-start.23 = (f32[1,896,896]{2,1,0:T(8,128)S(1)}, f32[1,896,896]{2,1,0:T(8,128)}, u32[]{:S(2)}) copy-start(f32[1,896,896]{2,1,0:T(8,128)} %param.45) | copy-start | bytes 9633796
  915.0 11.7 %copy-start.24 = (f32[1,896,896]{2,1,0:T(8,128)S(1)}, f32[1,896,896]{2,1,0:T(8,128)}, u32[]{:S(2)}) copy-start(f32[1,896,896]{2,1,0:T(8,128)} %param.52) | copy-start | bytes 9633796
  915.0 12.6 %copy-start.25 = (f32[896,896]{1,0:T(8,128)S(1)}, f32[896,896]{1,0:T(8,128)}, u32[]{:S(2)}) copy-start(f32[896,896]{1,0:T(8,128)} %get-tuple-element.386) | copy-start | bytes 9633796
  927.6 5.4 copy-start.5
  927.6 5.7 copy-start.6
  927.6 7.1 copy-start.28
  927.6 8.1 copy-start.29
  935.6 5.4 copy-start.74
  935.6 5.4 copy-start.82
  935.6 5.4 copy-start.83
  935.6 6.1 copy-start.3
  935.6 6.0 copy-start.27
  935.7 6.0 copy-start.44
  935.7 6.0 copy-start.45
  935.7 7.9 copy-start.33
  (38 other events, 83.7 us)
Sparse Core Ops, SparseCore 0:
  132.5 41.9 reduce-scatter.5
  176.6 47.0 all-gather.8
  301.8 23.9 reduce-scatter.7
  329.1 60.3 all-gather.10
  451.3 144.6 reduce-scatter.9
  611.5 20.7 reduce-scatter.11
  708.4 40.3 all-gather.12
  751.3 105.0 reduce-scatter.13

commit v2 on v1

v2 whole, which is shorter than its diff:
```python
import functools
import math

import jax
import jax.numpy as jnp
import numpy as np
from jax import lax
from jax.experimental import pallas as pl
from jax.experimental.pallas import tpu as pltpu
from jax.sharding import PartitionSpec as P

HEAD_DIM = 64


NORM_EPS = 1e-05
CLIP_LIMIT = 0.05
BETA_ONE = 0.5
BETA_TWO = 0.5
ADAM_STEP = 10.0
ADAM_EPS = 1e-08
RATE_MATRIX = 0.03
RATE_GAIN = 0.3
DECAY_MATRIX = 0.1


def rms_scale(values, gain):
    return values * lax.rsqrt(jnp.mean(values * values, axis=-1, keepdims=True) + NORM_EPS) * gain


def rotary_tables(length):
    half = HEAD_DIM // 2
    inverse = 10000.0 ** (-np.arange(half, dtype=np.float32) / half)
    angle = np.arange(length, dtype=np.float32)[:, None] * inverse[None, :]
    cosine, sine = np.cos(angle), np.sin(angle)
    cosine = np.concatenate([cosine] * 4, axis=1).astype(np.float32)
    sine = np.concatenate([-sine, sine] * 2, axis=1).astype(np.float32)
    return jnp.asarray(cosine), jnp.asarray(sine)


def product(left, right):
    return jnp.dot(left, right, preferred_element_type=jnp.float32)


def left_product(left, right):
    return lax.dot_general(
        left, right, (((0,), (0,)), ((), ())), preferred_element_type=jnp.float32
    )


def right_product(left, right):
    return lax.dot_general(
        left, right, (((1,), (1,)), ((), ())), preferred_element_type=jnp.float32
    )


def adam_step(weight, grad, first, second, rate, decay):
    mean = BETA_ONE * first + (1.0 - BETA_ONE) * grad
    square = BETA_TWO * second + (1.0 - BETA_TWO) * grad * grad
    mean_hat = mean / (1.0 - BETA_ONE**ADAM_STEP)
    square_hat = square / (1.0 - BETA_TWO**ADAM_STEP)
    return (
        weight - rate * (mean_hat / (jnp.sqrt(square_hat) + ADAM_EPS) + decay * weight),
        mean,
        square,
    )


def one_hot(index, extent):
    return (index[..., None] == jnp.arange(extent, dtype=jnp.int32)).astype(jnp.bfloat16)


def exchange_kernel(groups, plan, *refs):
    count = len(plan)
    ins, outs = refs[:count], refs[count : 2 * count]
    sends, recvs = refs[2 * count : 3 * count], refs[3 * count : 4 * count]
    local = refs[4 * count]
    sizes = [math.prod(lax.axis_size(axis) for axis in axes) for axes in groups]
    places = []
    for axes in groups:
        place = lax.axis_index(axes[0])
        for axis in axes[1:]:
            place = place * lax.axis_size(axis) + lax.axis_index(axis)
        places.append(place)

    def device(group, index):
        axes = groups[group]
        if len(axes) == 1:
            return {axes[0]: index}
        inner = lax.axis_size(axes[1])
        return {axes[0]: index // inner, axes[1]: lax.rem(index, inner)}

    barrier = pltpu.get_barrier_semaphore()
    for group, size in enumerate(sizes):

        def greet(step, carry, group=group, size=size):
            peer = lax.rem(places[group] + step, size)
            pl.semaphore_signal(
                barrier,
                inc=1,
                device_id=device(group, peer),
                device_id_type=pl.DeviceIdType.MESH,
            )
            return carry

        lax.fori_loop(1, size, greet, 0)
    pl.semaphore_wait(barrier, sum(sizes) - len(sizes))

    def copy(item, step, arriving):
        group, shared = plan[item]
        size, place = sizes[group], places[group]
        peer = lax.rem(place + step, size)
        source = ins[item] if shared else ins[item].at[peer]
        slot = lax.rem(place + size - step, size) if arriving else place
        return pltpu.make_async_remote_copy(
            src_ref=source,
            dst_ref=outs[item].at[slot],
            send_sem=sends[item].at[step],
            recv_sem=recvs[item].at[step],
            device_id=device(group, peer),
            device_id_type=pl.DeviceIdType.MESH,
        )

    for item in range(count):

        def begin(step, carry, item=item):
            copy(item, step, False).start()
            return carry

        lax.fori_loop(1, sizes[plan[item][0]], begin, 0)
    own = []
    for item in range(count):
        group, shared = plan[item]
        source = ins[item] if shared else ins[item].at[places[group]]
        own.append(
            pltpu.make_async_copy(source, outs[item].at[places[group]], local.at[item])
        )
        own[-1].start()
    for item in range(count):
        own[item].wait()

        def finish(step, carry, item=item):
            copy(item, step, False).wait_send()
            copy(item, step, True).wait_recv()
            return carry

        lax.fori_loop(1, sizes[plan[item][0]], finish, 0)


def exchange(ident, *items):
    groups, plan, shapes, scratch = [], [], [], []
    for axes, array, shared in items:
        if axes not in groups:
            groups.append(axes)
        plan.append((groups.index(axes), shared))
        size = math.prod(lax.axis_size(axis) for axis in axes)
        shape = (size,) + array.shape if shared else array.shape
        shapes.append(jax.ShapeDtypeStruct(shape, array.dtype))
        scratch.append(pltpu.SemaphoreType.DMA((size,)))
    result = pl.pallas_call(
        functools.partial(exchange_kernel, groups, plan),
        out_shape=shapes,
        in_specs=[pl.BlockSpec(memory_space=pltpu.VMEM)] * len(items),
        out_specs=[pl.BlockSpec(memory_space=pltpu.VMEM)] * len(items),
        scratch_shapes=scratch + scratch + [pltpu.SemaphoreType.DMA((len(items),))],
        compiler_params=pltpu.CompilerParams(collective_id=ident, has_side_effects=True),
        name="exchange_%d" % ident,
    )(*(array for _, array, _ in items))
    return result[0] if len(items) == 1 else result


GATHER_ORDERS = ((0, 1, 2), (2, 0, 1), (1, 2, 0))


def chip_grid():
    group_mod, group_dp = lax.axis_size("mod"), lax.axis_size("dp")
    deep = math.gcd(group_mod, 4)
    return deep, group_mod // deep, group_dp // 2


def row_pieces(rows):
    part = rows // 64 * 16
    return (0, part), (part, rows - 2 * part), (rows - part, part)


def chip_place(sizes):
    mod, dp = lax.axis_index("mod"), lax.axis_index("dp")
    return [mod // sizes[1], lax.rem(mod, sizes[1]), dp // 2], lax.rem(dp, 2)


def chip_device(sizes, at, core):
    return {"mod": at[0] * sizes[1] + at[1], "dp": at[2] * 2 + core}


def shifted(sizes, at, axis, step):
    at = list(at)
    at[axis] = lax.rem(at[axis] + step, sizes[axis])
    return at


def greet_lines(sizes, at, core):
    barrier = pltpu.get_barrier_semaphore()
    targets = [chip_device(sizes, at, 1 - core)]
    for axis in range(3):
        for step in range(1, sizes[axis]):
            targets.append(chip_device(sizes, shifted(sizes, at, axis, step), core))
    for target in targets:
        pl.semaphore_signal(
            barrier, inc=1, device_id=target, device_id_type=pl.DeviceIdType.MESH
        )
    pl.semaphore_wait(barrier, len(targets))


def line_copies(sizes):
    return sum(len(GATHER_ORDERS) * (size - 1) for size in sizes)


def gather_kernel(sizes, rows, in_ref, out_ref, send, recv, pair_send, pair_recv, local):
    at, core = chip_place(sizes)
    greet_lines(sizes, at, core)
    pieces = row_pieces(rows)
    keys = {}
    for piece, order in enumerate(GATHER_ORDERS):
        for stage, axis in enumerate(order):
            for step in range(1, sizes[axis]):
                keys[piece, stage, step] = len(keys)

    def region(at, done, core, piece):
        start, count = pieces[piece]
        index = tuple(slice(None) if axis in done else at[axis] for axis in range(3))
        return out_ref.at[index + (core, pl.ds(start, count))]

    def remote(source, target, sems, index, at, core):
        return pltpu.make_async_remote_copy(
            src_ref=source,
            dst_ref=target,
            send_sem=sems[0].at[index],
            recv_sem=sems[1].at[index],
            device_id=chip_device(sizes, at, core),
            device_id_type=pl.DeviceIdType.MESH,
        )

    def line(piece, stage, step, arriving):
        order = GATHER_ORDERS[piece]
        axis, done = order[stage], order[:stage]
        peer = shifted(sizes, at, axis, step)
        origin = shifted(sizes, at, axis, sizes[axis] - step)
        target = region(origin if arriving else at, done, core, piece)
        source = region(at, done, core, piece)
        if stage == 0:
            source = in_ref.at[pl.ds(*pieces[piece])]
        return remote(source, target, (send, recv), keys[piece, stage, step], peer, core)

    def pair(piece, stage, step, arriving):
        order = GATHER_ORDERS[piece]
        axis, done = order[stage], order[:stage]
        origin = shifted(sizes, at, axis, sizes[axis] - step)
        source = region(origin, done, core, piece)
        target = region(origin, done, 1 - core if arriving else core, piece)
        index = keys[piece, stage, step]
        return remote(source, target, (pair_send, pair_recv), index, at, 1 - core)

    def pair_own(arriving):
        target = out_ref.at[at[0], at[1], at[2], 1 - core if arriving else core]
        return remote(in_ref, target, (pair_send, pair_recv), len(keys), at, 1 - core)

    own = pltpu.make_async_copy(in_ref, out_ref.at[at[0], at[1], at[2], core], local)
    own.start()
    pair_own(False).start()
    for stage in range(4):
        for piece, order in enumerate(GATHER_ORDERS):
            if stage > 0:
                for step in range(1, sizes[order[stage - 1]]):
                    line(piece, stage - 1, step, True).wait_recv()
                if stage == 1 and piece == 0:
                    own.wait()
            if stage < 3:
                for step in range(1, sizes[order[stage]]):
                    line(piece, stage, step, False).start()
            if stage > 0:
                for step in range(1, sizes[order[stage - 1]]):
                    pair(piece, stage - 1, step, False).start()
    for piece, stage, step in keys:
        line(piece, stage, step, False).wait_send()
        pair(piece, stage, step, False).wait_send()
        pair(piece, stage, step, True).wait_recv()
    pair_own(False).wait_send()
    pair_own(True).wait_recv()


def gather_rows(ident, rows):
    sizes = chip_grid()
    count, width = rows.shape
    copies = line_copies(sizes)
    dma = pltpu.SemaphoreType.DMA
    gathered = pl.pallas_call(
        functools.partial(gather_kernel, sizes, count),
        out_shape=jax.ShapeDtypeStruct(sizes + (2, count, width), rows.dtype),
        in_specs=[pl.BlockSpec(memory_space=pltpu.VMEM)],
        out_specs=pl.BlockSpec(memory_space=pl.ANY),
        scratch_shapes=[dma((copies,)), dma((copies,)), dma((copies + 1,)), dma((copies + 1,)), dma],
        compiler_params=pltpu.CompilerParams(collective_id=ident, has_side_effects=True),
        name="gather_rows",
    )(rows)
    return gathered.reshape(-1, width)


def scatter_kernel(sizes, rows, in_ref, out_ref, acc, arrived, *rest):
    slots, (send, recv, pair_send, pair_recv, local) = rest[:-5], rest[-5:]
    at, core = chip_place(sizes)
    greet_lines(sizes, at, core)
    pieces = row_pieces(rows)
    orders = [order[::-1] for order in GATHER_ORDERS]
    keys = {}
    for piece, order in enumerate(orders):
        for stage, axis in enumerate(order):
            for step in range(1, sizes[axis]):
                keys[piece, stage, step] = len(keys)

    def line(piece, stage, step):
        order = orders[piece]
        axis, done = order[stage], order[:stage]
        peer = shifted(sizes, at, axis, step)
        index = tuple(
            peer[a] if a == axis else at[a] if a in done else slice(None) for a in range(3)
        )
        key = keys[piece, stage, step]
        return pltpu.make_async_remote_copy(
            src_ref=acc.at[index + (pl.ds(*pieces[piece]),)],
            dst_ref=slots[3 * piece + stage].at[step - 1],
            send_sem=send.at[key],
            recv_sem=recv.at[key],
            device_id=chip_device(sizes, peer, core),
            device_id_type=pl.DeviceIdType.MESH,
        )

    loads, pairs = [], []
    for piece in range(3):
        part = pl.ds(*pieces[piece])
        pairs.append(
            pltpu.make_async_remote_copy(
                src_ref=in_ref.at[:, :, :, 1 - core, part],
                dst_ref=arrived.at[:, :, :, part],
                send_sem=pair_send.at[piece],
                recv_sem=pair_recv.at[piece],
                device_id=chip_device(sizes, at, 1 - core),
                device_id_type=pl.DeviceIdType.MESH,
            )
        )
        pairs[-1].start()
        loads.append(
            pltpu.make_async_copy(
                in_ref.at[:, :, :, core, part], acc.at[:, :, :, part], local.at[piece]
            )
        )
        loads[-1].start()

    def add(piece, stage):
        order = orders[piece]
        done = order[:stage]
        left = [axis for axis in range(3) if axis not in done]
        part = pl.ds(*pieces[piece])

        def one(index, carry):
            where, inner = list(at), []
            for axis in reversed(left):
                where[axis] = lax.rem(index, sizes[axis])
                index = index // sizes[axis]
                inner.insert(0, where[axis])
            spot = tuple(where) + (part,)
            total = acc[spot].astype(jnp.float32)
            if stage == 0:
                total = total + arrived[spot].astype(jnp.float32)
            else:
                taken = slots[3 * piece + stage - 1]
                for step in range(taken.shape[0]):
                    total = total + taken[(step,) + tuple(inner)].astype(jnp.float32)
            if stage == 3:
                out_ref[part] = total
            else:
                acc[spot] = total.astype(acc.dtype)
            return carry

        lax.fori_loop(0, math.prod(sizes[axis] for axis in left), one, 0)

    for stage in range(4):
        for piece, order in enumerate(orders):
            if stage == 0:
                loads[piece].wait()
                pairs[piece].wait_recv()
            else:
                for step in range(1, sizes[order[stage - 1]]):
                    line(piece, stage - 1, step).wait_recv()
            add(piece, stage)
            if stage < 3:
                for step in range(1, sizes[order[stage]]):
                    line(piece, stage, step).start()
    for piece in range(3):
        pairs[piece].wait_send()
    for piece, stage, step in keys:
        line(piece, stage, step).wait_send()


def scatter_rows(ident, parts):
    sizes = chip_grid()
    width = parts.shape[1]
    count = parts.shape[0] // (2 * math.prod(sizes))
    copies = line_copies(sizes)
    dma = pltpu.SemaphoreType.DMA
    slots = []
    for piece, order in enumerate(GATHER_ORDERS):
        order = order[::-1]
        for stage, axis in enumerate(order):
            left = tuple(sizes[a] for a in range(3) if a not in order[: stage + 1])
            shape = (sizes[axis] - 1,) + left + (row_pieces(count)[piece][1], width)
            slots.append(pltpu.VMEM(shape, parts.dtype))
    return pl.pallas_call(
        functools.partial(scatter_kernel, sizes, count),
        out_shape=jax.ShapeDtypeStruct((count, width), jnp.float32),
        in_specs=[pl.BlockSpec(memory_space=pl.ANY)],
        out_specs=pl.BlockSpec(memory_space=pltpu.VMEM),
        scratch_shapes=[
            pltpu.VMEM(sizes + (count, width), parts.dtype),
            pltpu.VMEM(sizes + (count, width), parts.dtype),
            *slots,
            dma((copies,)),
            dma((copies,)),
            dma((3,)),
            dma((3,)),
            dma((3,)),
        ],
        compiler_params=pltpu.CompilerParams(collective_id=ident, has_side_effects=True),
        name="scatter_rows",
    )(parts.reshape(sizes + (2, count, width)))


GROUP_SEQS = 4


def wide_table(table_ref, tokens, width):
    table = table_ref[...]
    table = jnp.concatenate([table] * (tokens // table.shape[0]), axis=0)
    return jnp.concatenate([table] * (width // table.shape[1]), axis=1)


def turned(values, cosine, sine):
    width = values.shape[-1]
    half = HEAD_DIM // 2
    lane = lax.broadcasted_iota(jnp.int32, values.shape, 1)
    other = jnp.where(
        lane % HEAD_DIM < half,
        pltpu.roll(values, width - half, 1),
        pltpu.roll(values, half, 1),
    )
    return values * cosine + other * sine


def head_spread(values, heads):
    rows, width = values.shape
    lane = lax.broadcasted_iota(jnp.int32, (heads, rows, width), 2)
    head = lax.broadcasted_iota(jnp.int32, (heads, rows, width), 0)
    return jnp.where(lane // HEAD_DIM == head, values[None], jnp.zeros((), values.dtype))


def head_fold(values, heads):
    rows, width = values.shape
    values = values.reshape(heads, rows // heads, width)
    lane = lax.broadcasted_iota(jnp.int32, values.shape, 2)
    head = lax.broadcasted_iota(jnp.int32, values.shape, 0)
    return jnp.sum(jnp.where(lane // HEAD_DIM == head, values, 0.0), axis=0)


def attention_parts(length, spots_ref, mixed_ref, cosine_ref, sine_ref):
    tokens, width = mixed_ref.shape[0], mixed_ref.shape[1] // 3
    heads = width // HEAD_DIM
    cosine = wide_table(cosine_ref, tokens, width)
    sine = wide_table(sine_ref, tokens, width)
    spot = spots_ref[...]
    key = lax.broadcasted_iota(jnp.int32, (spot.shape[0], tokens), 1)
    chosen = key == spot
    seen = (key <= spot) & (key >= spot - spot % length)
    queries = turned(mixed_ref[:, :width], cosine, sine).astype(jnp.bfloat16)
    queries = product(chosen.astype(jnp.bfloat16), queries)
    queries = head_spread(queries, heads).reshape(-1, width).astype(jnp.bfloat16)
    keys_in = turned(mixed_ref[:, width : 2 * width], cosine, sine).astype(jnp.bfloat16)
    values = mixed_ref[:, 2 * width :].astype(jnp.bfloat16)
    raw = right_product(queries, keys_in).reshape(heads, -1, tokens)
    scores = jnp.where(seen[None], raw * HEAD_DIM ** (-0.5), -1e30).reshape(-1, tokens)
    top = jnp.max(scores, axis=1, keepdims=True)
    terms = jnp.exp(scores - top)
    chances = terms / jnp.sum(terms, axis=1, keepdims=True)
    return chosen, queries, keys_in, values, chances, cosine, sine


def attention_kernel(
    length, spots_ref, mixed_ref, inputs_ref, cosine_ref, sine_ref, heads_ref, picked_ref
):
    heads = inputs_ref.shape[1] // HEAD_DIM
    chosen, _, _, values, chances, _, _ = attention_parts(
        length, spots_ref, mixed_ref, cosine_ref, sine_ref
    )
    spread = product(chances.astype(jnp.bfloat16), values)
    heads_ref[...] = head_fold(spread, heads).astype(jnp.bfloat16)
    picked_ref[...] = product(chosen.astype(jnp.bfloat16), inputs_ref[...])


def attention_back_kernel(
    length, spots_ref, mixed_ref, grad_ref, cosine_ref, sine_ref, out_ref
):
    width = grad_ref.shape[1]
    heads = width // HEAD_DIM
    chosen, queries, keys_in, values, chances, cosine, sine = attention_parts(
        length, spots_ref, mixed_ref, cosine_ref, sine_ref
    )
    grad_heads = head_spread(grad_ref[...].astype(jnp.float32), heads)
    grad_heads = grad_heads.reshape(-1, width).astype(jnp.bfloat16)
    grad_values = left_product(chances.astype(jnp.bfloat16), grad_heads)
    grad_chances = right_product(grad_heads, values)
    delta = jnp.sum(chances * grad_chances, axis=1, keepdims=True)
    grad_raw = (chances * (grad_chances - delta) * HEAD_DIM ** (-0.5)).astype(jnp.bfloat16)
    grad_queries = head_fold(product(grad_raw, keys_in), heads)
    grad_queries = lax.dot_general(
        chosen.astype(jnp.float32),
        grad_queries,
        (((0,), (0,)), ((), ())),
        precision=lax.Precision.HIGHEST,
        preferred_element_type=jnp.float32,
    )
    grad_keys = left_product(grad_raw, queries)
    out_ref[:, :width] = turned(grad_queries, cosine, -sine).astype(jnp.bfloat16)
    out_ref[:, width : 2 * width] = turned(grad_keys, cosine, -sine).astype(jnp.bfloat16)
    out_ref[:, 2 * width :] = grad_values.astype(jnp.bfloat16)


def attention_call(body, length, operands, tables, outs, name):
    sequences = operands[1].shape[0] // length
    steps = sequences // math.gcd(GROUP_SEQS, sequences)

    def block(array):
        return pl.BlockSpec((array.shape[0] // steps, array.shape[1]), lambda i: (i, 0))

    fixed = [pl.BlockSpec(table.shape, lambda i: (0, 0)) for table in tables]
    return pl.pallas_call(
        functools.partial(body, length),
        grid=(steps,),
        out_shape=outs,
        in_specs=[block(array) for array in operands] + fixed,
        out_specs=[block(array) for array in outs],
        name=name,
    )(*operands, *tables)


def on_device(
    token_ids,
    targets,
    positions,
    loss_mask,
    paths,
    attend,
    output,
    widen,
    narrow,
    gains,
    table,
    final_gain,
    first_attend,
    first_output,
    first_widen,
    first_narrow,
    first_gains,
    first_table,
    first_final,
    second_attend,
    second_output,
    second_widen,
    second_narrow,
    second_gains,
    second_table,
    second_final,
):
    group_dp = lax.axis_size("dp")
    group_mod = lax.axis_size("mod")
    dp_place = lax.axis_index("dp")
    mod_place = lax.axis_index("mod")
    everyone = ("mod", "dp")
    place = mod_place * group_dp + dp_place
    sources = group_mod * group_dp
    micro, per_mod, length = token_ids.shape
    spots_seq = positions.shape[2]
    seq_dev = per_mod // group_dp
    shard_rows, width = table.shape
    heads = width // HEAD_DIM
    slots = micro * sources
    slots_local = slots // group_dp
    low = jnp.bfloat16

    mixing = lax.all_gather(
        jnp.concatenate([attend[0], output[0]], axis=1).astype(low), "dp", axis=0, tiled=True
    )
    attend_low, output_low = mixing[:, : 3 * width], mixing[:, 3 * width :]
    widen_low = lax.all_to_all(
        widen[0].astype(low), "dp", split_axis=1, concat_axis=0, tiled=True
    )
    narrow_low = narrow[0].astype(low)
    table_low = table.astype(low)

    fields = jnp.concatenate(
        [token_ids, positions, targets, loss_mask, paths[..., None]], axis=-1
    )
    fields, gain_parts, final_parts = exchange(
        0,
        (("mod",), fields.reshape(micro * per_mod, -1), True),
        (("dp",), jnp.broadcast_to(gains.astype(low), (16, gains.shape[1])), True),
        (("mod",), jnp.broadcast_to(final_gain.astype(low)[None], (16, final_gain.shape[0])), True),
    )
    own_gains = gain_parts[:, 0].reshape(-1).astype(jnp.float32)
    gain_one, gain_two = own_gains[:width], own_gains[width:]
    gain_final = final_parts[:, 0].reshape(-1).astype(jnp.float32)
    fields = fields.reshape(group_mod, micro, per_mod, -1).transpose(1, 0, 2, 3)
    fields = fields.reshape(slots, seq_dev, -1)
    own = lax.dynamic_slice_in_dim(fields, dp_place * slots_local, slots_local)
    own_match = own[..., -1] == mod_place
    own = jnp.sum(jnp.where(own_match[..., None], own[..., : length + spots_seq], 0), axis=1)
    own_tokens = own[:, :length].reshape(-1)
    spots = own[:, length:]
    held = jnp.repeat(jnp.any(own_match, axis=1), length)
    match = fields[None, ..., -1] == jnp.arange(group_mod, dtype=jnp.int32)[:, None, None]
    scoring = jnp.sum(
        jnp.where(match[..., None], fields[None, ..., length + spots_seq : -1], 0), axis=2
    )
    wanted = scoring[..., :spots_seq].reshape(-1)
    counted = scoring[..., spots_seq:].reshape(-1).astype(jnp.float32)
    count_total = jnp.sum(counted)

    shard = own_tokens // shard_rows
    row = own_tokens % shard_rows
    key = jnp.where(held, own_tokens, -1)
    order = jnp.arange(key.shape[0], dtype=jnp.int32)
    repeated = jnp.any((key[:, None] == key[None, :]) & (order[None, :] < order[:, None]), axis=1)
    leading = held & ~repeated
    rank = jnp.sum(
        (
            leading[None, :] & (shard[None, :] == shard[:, None]) & (key[None, :] < key[:, None])
        ).astype(jnp.int32),
        axis=1,
    )
    expected = -(-slots_local * length // sources)
    cap = -(-3 * expected // 16) * 8
    cap = min(max(cap, 16), -(-shard_rows // 8) * 8, 112)
    own_rounds = jnp.max(jnp.where(leading, rank // cap, 0)) + 1

    def ask(turn):
        slot = rank - turn * cap
        inside = held & (slot >= 0) & (slot < cap)
        slot = jnp.where(inside, shard * cap + slot, -1)
        asked = jnp.sum(
            jnp.where(
                leading[None, :]
                & (slot[None, :] == jnp.arange(sources * cap, dtype=jnp.int32)[:, None]),
                row[None, :] + 1,
                0,
            ),
            axis=1,
        ).reshape(sources, cap)
        return slot, asked

    slot, asked = ask(0)
    message = jnp.concatenate(
        [asked, jnp.broadcast_to(own_rounds, (sources, 128 - cap))], axis=1
    )
    message = exchange(
        1, (everyone, jnp.broadcast_to(message[:, None], (sources, 8, 128)), False)
    )
    rounds = jnp.max(message[:, 0, cap])
    spread = one_hot(slot, sources * cap)
    pick = one_hot(message[:, 0, :cap].reshape(-1) - 1, shard_rows)

    def other_plan(turn):
        slot, asked = ask(turn)
        asked = lax.all_to_all(asked, everyone, split_axis=0, concat_axis=0, tiled=True)
        return one_hot(slot, sources * cap), one_hot(asked.reshape(-1) - 1, shard_rows)

    def other_rows(state):
        turn, rows = state
        spread, pick = other_plan(turn)
        sent = product(pick, table_low).astype(low).reshape(sources, cap, width)
        got = lax.all_to_all(sent, everyone, split_axis=0, concat_axis=0, tiled=True)
        return turn + 1, rows + product(spread, got.reshape(-1, width)).astype(low)

    sent = product(pick, table_low).astype(low).reshape(sources, cap, width)
    got = exchange(2, (everyone, sent, False))
    inputs = product(spread, got.reshape(-1, width)).astype(low)
    inputs = lax.while_loop(
        lambda state: state[0] < rounds, other_rows, (jnp.int32(1), inputs)
    )[1]

    group = math.gcd(GROUP_SEQS, slots_local)
    tables = rotary_tables(length)
    flat_spots = spots + (jnp.arange(slots_local, dtype=jnp.int32) % group)[:, None] * length
    flat_spots = flat_spots.reshape(-1, 1)
    inputs_wide = inputs.astype(jnp.float32)
    normed_one = rms_scale(inputs_wide, gain_one).astype(low)
    mixed = product(normed_one, attend_low)
    picked_rows = slots_local * spots_seq
    heads_out, picked_inputs = attention_call(
        attention_kernel,
        length,
        (flat_spots, mixed, inputs),
        tables,
        [
            jax.ShapeDtypeStruct((picked_rows, width), low),
            jax.ShapeDtypeStruct((picked_rows, width), jnp.float32),
        ],
        "attention",
    )
    middle = picked_inputs + product(heads_out, output_low)

    def sum_parts(ident, parts):
        parts = parts.astype(low).reshape(group_dp, picked_rows, width)
        return jnp.sum(exchange(ident, (("dp",), parts, False)).astype(jnp.float32), axis=0)

    normed_two = rms_scale(middle, gain_two).astype(low)
    normed_all = exchange(3, (("dp",), normed_two, True)).reshape(-1, width)
    upper = product(normed_all, widen_low)
    gelu = lambda value: jax.nn.gelu(value, approximate=True)
    activated = gelu(upper).astype(low)
    lifted = sum_parts(4, product(activated, narrow_low))
    returned = (middle + lifted).astype(low).astype(jnp.float32)

    final, final_back = jax.vjp(rms_scale, returned, gain_final)
    scored = gather_rows(12, final.astype(low))
    logits = right_product(scored, table_low)
    target_row = wanted - place * shard_rows
    hits = target_row[:, None] == jnp.arange(shard_rows, dtype=jnp.int32)
    local_top = jnp.max(logits, axis=1)
    local_total = jnp.sum(jnp.exp(logits - local_top[:, None]), axis=1)
    local_target = jnp.sum(jnp.where(hits, logits, 0.0), axis=1)
    stats = jnp.stack(
        [part.reshape(sources, picked_rows) for part in (local_top, local_total, local_target)],
        axis=1,
    )
    stats = exchange(5, (everyone, jnp.pad(stats, ((0, 0), (0, 5), (0, 0))), False))
    top = jnp.max(stats[:, 0], axis=0)
    total = jnp.sum(stats[:, 1] * jnp.exp(stats[:, 0] - top), axis=0)
    own_totals = jnp.stack([top + jnp.log(total), jnp.sum(stats[:, 2], axis=0)])
    totals = exchange(6, (everyone, jnp.pad(own_totals, ((0, 6), (0, 0))), True))
    log_total = totals[:, 0].reshape(-1)
    loss_total = jnp.sum(counted * (log_total - totals[:, 1].reshape(-1)))
    grad_logits = (
        counted[:, None] * (jnp.exp(logits - log_total[:, None]) - hits.astype(jnp.float32))
    ).astype(low)
    table_grad = left_product(grad_logits, scored)
    grad_picked = scatter_rows(13, product(grad_logits, table_low).astype(low))

    grad_returned, grad_final = final_back(grad_picked)
    incoming = grad_returned.astype(low)
    incoming_all = exchange(7, (("dp",), incoming, True)).reshape(-1, width)
    grad_narrow = left_product(activated, incoming_all)
    grad_act = right_product(incoming_all, narrow_low)
    grad_upper = jax.vjp(gelu, upper)[1](grad_act)[0].astype(low)
    grad_widen = left_product(normed_all, grad_upper).astype(low)
    grad_widen = lax.all_to_all(grad_widen, "dp", split_axis=0, concat_axis=1, tiled=True)
    grad_widen = grad_widen.astype(jnp.float32)
    grad_normed_two = sum_parts(8, right_product(grad_upper, widen_low))
    grad_middle, grad_gain_two = jax.vjp(rms_scale, middle, gain_two)[1](grad_normed_two)
    grad_middle = grad_middle + incoming.astype(jnp.float32)

    branch_grad = grad_middle.astype(low)
    grad_output = left_product(heads_out, branch_grad)
    grad_heads = right_product(branch_grad, output_low).astype(low)
    (grad_mixed,) = attention_call(
        attention_back_kernel,
        length,
        (flat_spots, mixed, grad_heads),
        tables,
        [jax.ShapeDtypeStruct(mixed.shape, low)],
        "attention_back",
    )
    grad_attend = left_product(normed_one, grad_mixed)
    grad_normed = right_product(grad_mixed, attend_low)
    grad_inputs, grad_gain_one = jax.vjp(rms_scale, inputs_wide, gain_one)[1](grad_normed)
    here = spots[:, :, None] == jnp.arange(length, dtype=jnp.int32)
    grad_skip = jnp.sum(
        jnp.where(
            here[..., None], grad_middle.reshape(slots_local, spots_seq, 1, width), 0.0
        ),
        axis=1,
    ).reshape(-1, width)
    leaving = (grad_skip + grad_inputs).astype(low)

    grad_mixing = lax.psum_scatter(
        jnp.concatenate([grad_attend, grad_output], axis=1).astype(low),
        "dp",
        scatter_dimension=0,
        tiled=True,
    ).astype(jnp.float32)

    def other_grads(state):
        turn, total = state
        spread, pick = other_plan(turn)
        sent = left_product(spread, leaving).astype(low).reshape(sources, cap, width)
        got = lax.all_to_all(sent, everyone, split_axis=0, concat_axis=0, tiled=True)
        return turn + 1, total + left_product(pick, got.reshape(-1, width))

    given = left_product(spread, leaving).astype(low).reshape(sources, cap, width)
    given = exchange(9, (everyone, given, False))
    table_grad = table_grad + left_product(pick, given.reshape(-1, width))
    table_grad = lax.while_loop(
        lambda state: state[0] < rounds, other_grads, (jnp.int32(1), table_grad)
    )[1]
    gain_grads = jnp.concatenate([grad_gain_one, grad_gain_two, grad_final])
    gain_grads = jnp.pad(gain_grads.reshape(-1, 128), ((0, -gain_grads.shape[0] // 128 % 8), (0, 0)))
    gain_grads = jnp.sum(exchange(10, (("dp",), gain_grads, True)), axis=0).reshape(-1)
    own_gain_grads = gain_grads[: 2 * width]
    final_rows = gain_grads[2 * width : 3 * width].reshape(-1, 128)
    gain_part = gains.shape[1]
    grad_gains = lax.dynamic_slice_in_dim(own_gain_grads, dp_place * gain_part, gain_part)
    matrix_grads = (
        grad_mixing[None, :, : 3 * width],
        grad_mixing[None, :, 3 * width :],
        grad_widen[None],
        grad_narrow[None],
    )
    squares = sum((jnp.sum(g * g) for g in matrix_grads)) + jnp.sum(table_grad * table_grad)
    squares = squares + jnp.sum(grad_gains * grad_gains)
    last = jnp.concatenate(
        [final_rows, jnp.broadcast_to(squares, (16 - final_rows.shape[0] % 8 - 8, 128))], axis=0
    )
    last = exchange(11, (everyone, last, True))
    final_count = final_rows.shape[0]
    grad_final = (
        jnp.sum(last[:, :final_count].reshape(group_mod, group_dp, -1)[:, 0], axis=0)
    )
    squares = jnp.sum(last[:, final_count, 0]) + jnp.sum(grad_final * grad_final)
    final_part = final_gain.shape[0]
    grad_final = lax.dynamic_slice_in_dim(grad_final, mod_place * final_part, final_part)
    gradient_norm = jnp.sqrt(squares) / count_total
    factor = CLIP_LIMIT / jnp.maximum(gradient_norm, CLIP_LIMIT) / count_total
    params = (attend, output, widen, narrow, gains, table, final_gain)
    grads = matrix_grads + (grad_gains[None], table_grad, grad_final)
    firsts = (
        first_attend,
        first_output,
        first_widen,
        first_narrow,
        first_gains,
        first_table,
        first_final,
    )
    seconds = (
        second_attend,
        second_output,
        second_widen,
        second_narrow,
        second_gains,
        second_table,
        second_final,
    )
    rates = (RATE_MATRIX, RATE_MATRIX, RATE_MATRIX, RATE_MATRIX, RATE_GAIN, RATE_MATRIX, RATE_GAIN)
    decays = (DECAY_MATRIX, DECAY_MATRIX, DECAY_MATRIX, DECAY_MATRIX, 0.0, DECAY_MATRIX, 0.0)
    updated = [
        adam_step(w, g * factor, f, s, r, c)
        for w, g, f, s, r, c in zip(params, grads, firsts, seconds, rates, decays)
    ]
    return (
        loss_total / count_total,
        gradient_norm,
        *(entry[0] for entry in updated),
        *(entry[1] for entry in updated),
        *(entry[2] for entry in updated),
    )


def solution(mesh):
    placed = (
        P(None, "mod", None),
        P(None, "mod", None),
        P(None, "mod", None),
        P(None, "mod", None),
        P(None, "mod"),
        P("mod", "dp", None),
        P("mod", "dp", None),
        P("mod", "dp", None),
        P("mod", "dp", None),
        P("mod", "dp"),
        P(("mod", "dp"), None),
        P("mod"),
        P("mod", "dp", None),
        P("mod", "dp", None),
        P("mod", "dp", None),
        P("mod", "dp", None),
        P("mod", "dp"),
        P(("mod", "dp"), None),
        P("mod"),
        P("mod", "dp", None),
        P("mod", "dp", None),
        P("mod", "dp", None),
        P("mod", "dp", None),
        P("mod", "dp"),
        P(("mod", "dp"), None),
        P("mod"),
    )
    return jax.shard_map(
        on_device,
        mesh=mesh,
        in_specs=placed,
        out_specs=(
            P(),
            P(),
            P("mod", "dp", None),
            P("mod", "dp", None),
            P("mod", "dp", None),
            P("mod", "dp", None),
            P("mod", "dp"),
            P(("mod", "dp"), None),
            P("mod"),
            P("mod", "dp", None),
            P("mod", "dp", None),
            P("mod", "dp", None),
            P("mod", "dp", None),
            P("mod", "dp"),
            P(("mod", "dp"), None),
            P("mod"),
            P("mod", "dp", None),
            P("mod", "dp", None),
            P("mod", "dp", None),
            P("mod", "dp", None),
            P("mod", "dp"),
            P(("mod", "dp"), None),
            P("mod"),
        ),
        check_vma=False,
    )
```

time: 970 us -> 535 us (0.55)
  waiting for transfers between devices: 325 us -> 0.06 us
  Pallas kernels: 0 us -> 277 us
  blocking collectives: 266 us -> 0 us
  matrix products: 127 us -> 82.8 us
  local copies, waits for them, and re-layouts: 70.8 us -> 38.7 us
  other arithmetic: 117 us -> 88.8 us
  starting transfers between devices: 23.4 us -> 8.39 us
    pallas_call x0 -> x16, Pallas kernels: none -> 277 us  [the longest x12 185 us: exchange(): pl.pallas_call(functools.partial(exchange_kernel, groups, plan), out_shap...]
    reduce_scatter x5 -> x1, waiting for transfers between devices: 186 us -> 0.01 us  [on_device(): lax.psum_scatter(jnp.concatenate([grad_attend, grad_output], axis=1).asty...]
    all_gather x6 -> x0, blocking collectives: 184 us -> none  [the longest x1 43.2 us: on_device(): lax.all_gather(jnp.concatenate([grad_gain_one, grad_gain_two, grad_final]...]
    all_gather x2 -> x0, waiting for transfers between devices: 82.3 us -> none  [the longest x1 59.9 us: on_device(): lax.all_gather(final.astype(low), ('mod', 'dp'), axis=0, tiled=True)]
    pmax x1 -> x0, blocking collectives: 43 us -> none  [on_device(): lax.pmax(jnp.max(jnp.where(leading, rank // cap, 0)) + 1, ('mod', 'dp'))]
    dot_general x9 -> x0, matrix products: 40.4 us -> none  [the longest x1 14.1 us: on_device(): jnp.einsum('shkt,skhe->sthe', grad_raw, queries, preferred_element_type=j...]
    psum x1 -> x0, blocking collectives: 39 us -> none  [on_device(): gradient_norm = jnp.sqrt(lax.psum(squares, ('mod', 'dp'))) / count_total]
    all_gather x1, waiting for transfers between devices: 36.8 us -> 0.02 us  [on_device(): lax.all_gather(jnp.concatenate([attend[0], output[0]], axis=1).astype(low...]
  transfers between devices with their start and end apart: 13 -> 4, of which waited for: 8 -> 0; matrix products, arithmetic and copies ran while one was open for 8% -> 15% of each run, Pallas kernels for 0% -> 25%
where the time goes in v2:
time: 535 us; the launch traced here: 524 us
  Pallas kernels  277 us (52%)
  other arithmetic  88.8 us (17%)
  matrix products  82.8 us (15%)
  local copies, waits for them, and re-layouts  38.7 us (7%)
  between operations  26.5 us (5%)
  starting transfers between devices  8.39 us (2%)
    pallas_call x12, Pallas kernels, exchange(): pl.pallas_call(functools.partial(exchange_kernel, groups, plan), out_shap...  185 us
    pallas_call x1, Pallas kernels, gather_rows(): pl.pallas_call(functools.partial(gather_kernel, sizes, count), out_shape=...  38.2 us
    pallas_call x1, Pallas kernels, scatter_rows(): pl.pallas_call(functools.partial(scatter_kernel, sizes, count), out_shape...  34.1 us
    dot_general x7, matrix products, product(): return jnp.dot(left, right, preferred_element_type=jnp.float32)  29.3 us
    sub x7, other arithmetic, adam_step(): weight - rate * (mean_hat / (jnp.sqrt(square_hat) + ADAM_EPS) + decay * w...  28.8 us
    dot_general x7, matrix products, left_product(): lax.dot_general(left, right, (((0,), (0,)), ((), ())), preferred_element_...  26.9 us
    dot_general x5, matrix products, right_product(): lax.dot_general(left, right, (((1,), (1,)), ((), ())), preferred_element_...  26.5 us
    pallas_call x2, Pallas kernels, attention_call(): pl.pallas_call(functools.partial(body, length), grid=(steps,), out_shape=...  19.7 us
  transfers between devices with their start and end apart: 4, of which 0 were waited for; matrix products, arithmetic and copies ran while one was open for 15% of the time, Pallas kernels for 25%

profile of v2, /device:TPU:0, one launch (start us, length us, event | category | flops | bytes accessed | tf_op | source)
XLA Modules:
  0.0 524.2 jit_solution(15407515077607624178)
XLA Ops:
  7.2 1.9 convert_bitcast_fusion
  12.9 14.1 %exchange_0.1 = (s32[8,48,45]{2,1,0:T(8,128)}, bf16[4,16,448]{2,1,0:T(8,128)(2,1)}, bf16[8,16,112]{2,1,0:T(8,128)(2,1)}) custom-call(s32[48,45]{1,0:T(8,128)} %concatenate.43.refs_0_, bf16[16,448]{1,0:T(8,128)(2,1)} %broadcast_in_dim.152.refs_1_, bf16[16,112]{1,0:T(8,128)(2,1)} %broadcast_in_dim.216.refs_2_), custom_call_target="tpu_custom_call" | custom-call | tf_op jit(solution)/shard_map/exchange_0/pallas_call | solution.py:159
  33.2 9.9 %exchange_1.1 = s32[32,8,128]{2,1,0:T(8,128)} custom-call(s32[32,8,128]{2,1,0:T(8,128)} %broadcast_in_dim.227.refs_0_), custom_call_target="tpu_custom_call" | custom-call | tf_op jit(solution)/shard_map/exchange_1/pallas_call | solution.py:159
  44.2 2.2 convert_element_type.182
  46.4 2.9 fusion.42
  49.4 30.4 %exchange_2.1 = bf16[32,24,896]{2,1,0:T(8,128)(2,1)} custom-call(bf16[32,24,896]{2,1,0:T(8,128)(2,1)} %bitcast.152), custom_call_target="tpu_custom_call" | custom-call | tf_op jit(solution)/shard_map/exchange_2/pallas_call | solution.py:159
  83.4 3.1 convert_element_type.190
  92.1 1.6 slice_reduce_fusion.3
  93.7 2.3 fusion.51
  97.3 4.4 all-to-all-start.4
  101.8 7.4 %fusion.19.mixed_ref = f32[512,2688]{1,0:T(8,128)} fusion(bf16[896,3584]{1,0:T(8,128)(2,1)} %all-gather.2.cloned.1.call-done, bf16[512,896]{1,0:T(8,128)(2,1)S(1)} %get-tuple-element.261.inputs_ref, f32[896]{0:T(1024)S(1)} %slice.106, f32[512]{0:T(512)S(1)} %fusion.100), kind=kOutput, calls=%fused_computation.45 | convolution fusion | flops 2468085760 | bytes 11245056 | tf_op jit(solution)/shard_map/dot_general | solution.py:41
  109.3 7.1 %attention.1 = (bf16[64,896]{1,0:T(8,128)(2,1)}, f32[64,896]{1,0:T(8,128)}) custom-call(s32[64,1]{1,0:T(8,128)} %reshape.607.spots_ref, f32[512,2688]{1,0:T(8,128)} %fusion.19.mixed_ref, bf16[512,896]{1,0:T(8,128)(2,1)S(1)} %get-tuple-element.261.inputs_ref, f32[32,128]{1,0:T(8,128)} %constant.222.clone.cosine_ref, f32[32,128]{1,0:T(8,128)} %constant.223.clone.sine_ref), custom_call_target="tpu_custom_call" | custom-call | tf_op jit(solution)/shard_map/attention/pallas_call | solution.py:542
  116.3 2.1 multiply_reduce_fusion.6
  119.2 9.1 %exchange_3.1 = bf16[4,64,896]{2,1,0:T(8,128)(2,1)} custom-call(bf16[64,896]{1,0:T(8,128)(2,1)} %multiply_convert_fusion.2.refs_0_), custom_call_target="tpu_custom_call" | custom-call | tf_op jit(solution)/shard_map/exchange_3/pallas_call | solution.py:159
  128.3 2.3 fusion.121
  131.5 1.5 fusion.56
  133.1 9.2 %exchange_4.1 = bf16[4,64,896]{2,1,0:T(8,128)(2,1)} custom-call(bf16[4,64,896]{2,1,0:T(8,128)(2,1)} %bitcast.147), custom_call_target="tpu_custom_call" | custom-call | tf_op jit(solution)/shard_map/exchange_4/pallas_call | solution.py:159
  144.5 1.4 fusion.87.in_ref
  146.0 38.2 %gather_rows.1 = bf16[4,2,2,2,64,896]{5,4,3,2,1,0:T(8,128)(2,1)} custom-call(bf16[64,896]{1,0:T(8,128)(2,1)} %fusion.87.in_ref), custom_call_target="tpu_custom_call" | custom-call | tf_op jit(solution)/shard_map/gather_rows/pallas_call | solution.py:295
  184.2 10.8 %fusion.120 = (f32[2048]{0:T(1024)}, f32[2048,1000]{0,1:T(8,128)}) fusion(bf16[2048,896]{1,0:T(8,128)(2,1)} %bitcast.144, bf16[1000,896]{1,0:T(8,128)(2,1)} %get-tuple-element.603), kind=kOutput, calls=%fused_computation.241 | convolution fusion | flops 3672061952 | bytes 13662208 | tf_op jit(solution)/shard_map/dot_general | solution.py:51
  195.0 1.4 stack_reshape.9
  196.4 5.2 exponential_reduce_fusion
  201.5 1.4 stack_reshape.10
  204.3 1.5 select_maximum_fusion.refs_0_
  205.7 13.5 %exchange_5.1 = f32[32,8,64]{2,1,0:T(8,128)} custom-call(f32[32,8,64]{2,1,0:T(8,128)} %select_maximum_fusion.refs_0_), custom_call_target="tpu_custom_call" | custom-call | tf_op jit(solution)/shard_map/exchange_5/pallas_call | solution.py:159
  219.2 2.2 fusion.118
  225.4 10.2 %exchange_6.1 = f32[32,8,64]{2,1,0:T(8,128)} custom-call(f32[8,64]{1,0:T(8,128)} %select_maximum_fusion.4.refs_0_), custom_call_target="tpu_custom_call" | custom-call | tf_op jit(solution)/shard_map/exchange_6/pallas_call | solution.py:159
  235.6 1.7 slice_reduce_fusion.4
  237.2 1.4 sub.151
  238.6 10.7 %convolution_convert_fusion.2 = bf16[2048,896]{1,0:T(8,128)(2,1)} fusion(bf16[1000,896]{1,0:T(8,128)(2,1)} %get-tuple-element.603, f32[2048,1000]{0,1:T(8,128)} %get-tuple-element.406, f32[2048]{0:T(1024)} %sub.151, f32[2048]{0:T(1024)} %convert_element_type.201, s32[2048]{0:T(1024)} %sub.146), kind=kOutput, calls=%fused_computation.49 | convolution fusion | flops 3684139008 | bytes 13678592 | tf_op jit(solution)/shard_map/dot_general | solution.py:41
  249.4 34.1 %scatter_rows.1 = f32[64,896]{1,0:T(8,128)} custom-call(bf16[4,2,2,2,64,896]{5,4,3,2,1,0:T(8,128)(2,1)} %bitcast.146), custom_call_target="tpu_custom_call" | custom-call | tf_op jit(solution)/shard_map/scatter_rows/pallas_call | solution.py:416
  283.4 1.7 fusion.92
  285.7 1.7 fusion.89.refs_0_
  287.5 8.5 %exchange_7.1 = bf16[4,64,896]{2,1,0:T(8,128)(2,1)} custom-call(bf16[64,896]{1,0:T(8,128)(2,1)} %fusion.89.refs_0_), custom_call_target="tpu_custom_call" | custom-call | tf_op jit(solution)/shard_map/exchange_7/pallas_call | solution.py:159
  296.0 2.5 fusion.73
  299.3 3.0 convolution_convert_fusion.6
  302.2 9.2 %exchange_8.1 = bf16[4,64,896]{2,1,0:T(8,128)(2,1)} custom-call(bf16[4,64,896]{2,1,0:T(8,128)(2,1)} %bitcast.155), custom_call_target="tpu_custom_call" | custom-call | tf_op jit(solution)/shard_map/exchange_8/pallas_call | solution.py:159
  313.5 2.7 fusion.62.grad_ref
  316.2 12.6 %attention_back.1 = bf16[512,2688]{1,0:T(8,128)(2,1)} custom-call(s32[64,1]{1,0:T(8,128)} %reshape.607.spots_ref, f32[512,2688]{1,0:T(8,128)} %fusion.19.mixed_ref, bf16[64,896]{1,0:T(8,128)(2,1)} %fusion.62.grad_ref, f32[32,128]{1,0:T(8,128)} %constant.222.clone.cosine_ref, f32[32,128]{1,0:T(8,128)} %constant.223.clone.sine_ref), custom_call_target="tpu_custom_call" | custom-call | tf_op jit(solution)/shard_map/attention_back/pallas_call | solution.py:542
  328.8 6.9 %convolution_convert_fusion.1 = bf16[896,2688]{1,0:T(8,128)(2,1)} fusion(bf16[512,2688]{1,0:T(8,128)(2,1)} %attention_back.1, bf16[512,896]{1,0:T(8,128)(2,1)S(1)} %copy-done.8, f32[896]{0:T(1024)S(1)} %copy-done.52, f32[512]{0:T(512)S(1)} %copy-done.54), kind=kOutput, calls=%fused_computation.36 | convolution fusion | flops 2470494208 | bytes 8492544 | tf_op jit(solution)/shard_map/dot_general | solution.py:45
  335.7 5.5 %pad_maximum_fusion = bf16[896,3584]{1,0:T(8,128)(2,1)} fusion(bf16[896,896]{1,0:T(8,128)(2,1)S(1)} %convolution_convert_fusion.4, bf16[896,2688]{1,0:T(8,128)(2,1)} %convolution_convert_fusion.1), kind=kLoop, calls=%fused_computation.35 | loop fusion | flops 12845056 | bytes 12845056 | tf_op jit(solution)/shard_map/concatenate | solution.py:791
  342.1 7.6 %fusion.40 = (f32[512]{0:T(512)S(1)}, f32[896]{0:T(1024)S(1)}, f32[512,896]{1,0:T(8,128)S(1)}) fusion(bf16[512,896]{1,0:T(8,128)(2,1)S(1)} %copy-done.8, f32[896]{0:T(1024)S(1)} %copy-done.52, f32[512]{0:T(512)S(1)} %copy-done.54, bf16[512,2688]{1,0:T(8,128)(2,1)} %attention_back.1, bf16[896,3584]{1,0:T(8,128)(2,1)} %all-gather.2.cloned.1.call-done), kind=kOutput, calls=%fused_computation.85 | convolution fusion | flops 2469460480 | bytes 10333184 | tf_op jit(solution)/shard_map/dot_general | solution.py:51
  351.6 2.2 convolution_convert_fusion.5
  353.7 32.5 %exchange_9.1 = bf16[32,24,896]{2,1,0:T(8,128)(2,1)} custom-call(bf16[32,24,896]{2,1,0:T(8,128)(2,1)} %bitcast.151), custom_call_target="tpu_custom_call" | custom-call | tf_op jit(solution)/shard_map/exchange_9/pallas_call | solution.py:159
  386.3 1.8 convolution_convert_fusion.3
  388.2 8.5 %fusion.107 = f32[1000,896]{1,0:T(8,128)S(1)} fusion(bf16[2048,896]{1,0:T(8,128)(2,1)} %bitcast.145, f32[2048,1000]{0,1:T(8,128)} %get-tuple-element.406, f32[2048]{0:T(1024)S(1)} %copy-done.56, f32[2048]{0:T(1024)S(1)} %copy-done.55, s32[2048]{0:T(1024)S(1)} %copy-done.46), kind=kOutput, calls=%fused_computation.237 | convolution fusion | flops 3682304000 | bytes 15470592 | tf_op jit(solution)/shard_map/dot_general | solution.py:45
  396.7 3.8 fusion.41
  401.2 3.9 all-to-all-start.5
  405.8 26.7 %exchange_10.1 = f32[4,24,128]{2,1,0:T(8,128)} custom-call(f32[24,128]{1,0:T(8,128)} %select_maximum_fusion.2.refs_0_), custom_call_target="tpu_custom_call" | custom-call | tf_op jit(solution)/shard_map/exchange_10/pallas_call | solution.py:159
  436.3 3.5 multiply_reduce_fusion
  439.9 3.1 multiply_reduce_fusion.1
  443.0 1.4 fusion.22
  444.4 1.8 convert_element_type.212
  452.7 12.1 %exchange_11.1 = f32[32,8,128]{2,1,0:T(8,128)} custom-call(f32[8,128]{1,0:T(8,128)} %concatenate.51.refs_0_), custom_call_target="tpu_custom_call" | custom-call | tf_op jit(solution)/shard_map/exchange_11/pallas_call | solution.py:159
  464.8 1.5 slice_reduce_fusion.1
  470.7 1.6 fusion.23
  472.3 3.8 copy.146
  476.1 4.9 mul.722
  481.0 8.9 %multiply_subtract_fusion = (f32[1000,896]{1,0:T(8,128)}, f32[1000,896]{1,0:T(8,128)}, f32[1000,896]{1,0:T(8,128)}) fusion(f32[1000,896]{1,0:T(8,128)} %param.42, f32[1000,896]{1,0:T(8,128)} %get-tuple-element.266, f32[]{:T(128)S(6)} %div.152, f32[1000,896]{1,0:T(8,128)} %param.49, f32[1000,896]{1,0:T(8,128)} %param.56), kind=kLoop, calls=%fused_computation.51 | loop fusion | flops 13440000 | bytes 25088004 | tf_op jit(solution)/shard_map/sub | solution.py:62
  490.0 1.9 multiply_subtract_fusion.4
  493.3 6.5 %multiply_subtract_fusion.3 = (f32[1,224,2688]{2,1,0:T(8,128)}, f32[1,224,2688]{2,1,0:T(8,128)}, f32[1,224,2688]{2,1,0:T(8,128)}) fusion(f32[1,224,2688]{2,1,0:T(8,128)S(1)} %copy-done.6, f32[]{:T(128)S(6)} %div.152, f32[224,3584]{1,0:T(8,128)S(1)} %convert_element_type.212, f32[1,224,2688]{2,1,0:T(8,128)S(1)} %copy-done.19, f32[1,224,2688]{2,1,0:T(8,128)} %param.51), kind=kLoop, calls=%fused_computation.75 | loop fusion | flops 9031680 | bytes 16859140 | tf_op jit(solution)/shard_map/sub | solution.py:62
  501.3 5.7 %multiply_subtract_fusion.1 = (f32[1,896,896]{2,1,0:T(8,128)}, f32[1,896,896]{2,1,0:T(8,128)}, f32[1,896,896]{2,1,0:T(8,128)}) fusion(f32[1,896,896]{2,1,0:T(8,128)S(1)} %copy-done.2, f32[896,896]{1,0:T(8,128)S(1)} %copy-done.14, f32[]{:T(128)S(6)} %div.152, f32[1,896,896]{2,1,0:T(8,128)S(1)} %copy-done.12, f32[1,896,896]{2,1,0:T(8,128)S(1)} %copy-done.13), kind=kLoop, calls=%fused_computation.61 | loop fusion | flops 12042240 | bytes 22478852 | tf_op jit(solution)/shard_map/sub | solution.py:62
  507.0 1.5 copy-done.17
  509.4 4.6 multiply_subtract_fusion.2
  (260 shorter events, 48.5 us)
Async XLA Ops:
  7.2 94.6 %all-gather.2.cloned.1.call-start = ((), (), s32[]{:S(2)}) async-start(), calls=%async_computation.7 | async-start | bytes 8028160 | tf_op jit(solution)/shard_map/all_gather | solution.py:596
  31.4 62.3 %copy-start.57 = (s32[512]{0:T(512)}, s32[512]{0:T(512)S(1)}, u32[]{:S(2)}) copy-start(s32[512]{0:T(512)S(1)} %get-tuple-element.402) | copy-start | bytes 6148
  44.2 5.2 copy-start.67
  46.4 35.7 %copy-start.3 = (f32[1,224,3584]{2,1,0:T(8,128)S(1)}, f32[1,224,3584]{2,1,0:T(8,128)}, u32[]{:S(2)}) copy-start(f32[1,224,3584]{2,1,0:T(8,128)} %param.39) | copy-start | bytes 9633796
  80.7 21.1 %copy-start.51 = (f32[896]{0:T(1024)}, f32[896]{0:T(1024)S(1)}, u32[]{:S(2)}) copy-start(f32[896]{0:T(1024)S(1)} %slice.106) | copy-start | bytes 10756
  82.1 36.3 %copy-start.42 = (f32[896]{0:T(1024)}, f32[896]{0:T(1024)S(1)}, u32[]{:S(2)}) copy-start(f32[896]{0:T(1024)S(1)} %slice.110) | copy-start | bytes 10756
  83.4 5.8 %copy-start.22 = (s32[64,6,8]{2,1,0:T(8,128)S(1)}, s32[64,6,8]{2,1,0:T(8,128)}, u32[]{:S(2)}) copy-start(s32[64,6,8]{2,1,0:T(8,128)} %slice.127) | copy-start | bytes 36868
  97.0 12.3 %copy-start.7 = (bf16[512,896]{1,0:T(8,128)(2,1)}, bf16[512,896]{1,0:T(8,128)(2,1)S(1)}, u32[]{:S(2)}) copy-start(bf16[512,896]{1,0:T(8,128)(2,1)S(1)} %get-tuple-element.261.inputs_ref) | copy-start | bytes 2752516
  97.0 12.2 %copy-start.30 = (s32[512]{0:T(512)}, s32[512]{0:T(512)S(1)}, u32[]{:S(2)}) copy-start(s32[512]{0:T(512)S(1)} %get-tuple-element.607) | copy-start | bytes 6148
  97.0 12.2 %copy-start.32 = (s32[512]{0:T(512)}, s32[512]{0:T(512)S(1)}, u32[]{:S(2)}) copy-start(s32[512]{0:T(512)S(1)} %get-tuple-element.608) | copy-start | bytes 6148
  97.0 12.2 %copy-start.34 = (s32[512]{0:T(512)}, s32[512]{0:T(512)S(1)}, u32[]{:S(2)}) copy-start(s32[512]{0:T(512)S(1)} %get-tuple-element.609) | copy-start | bytes 6148
  97.0 12.2 %copy-start.38 = (pred[512]{0:T(512)(128)(4,1)}, pred[512]{0:T(512)(128)(4,1)S(1)}, u32[]{:S(2)}) copy-start(pred[512]{0:T(512)(128)(4,1)S(1)} %get-tuple-element.610) | copy-start | bytes 1540
  97.0 12.2 %copy-start.40 = (pred[16]{0:T(512)(128)(4,1)}, pred[16]{0:T(512)(128)(4,1)S(1)}, u32[]{:S(2)}) copy-start(pred[16]{0:T(512)(128)(4,1)S(1)} %get-tuple-element.611) | copy-start | bytes 52
  97.3 12.0 %copy-start.48 = (f32[512]{0:T(512)}, f32[512]{0:T(512)S(1)}, u32[]{:S(2)}) copy-start(f32[512]{0:T(512)S(1)} %fusion.39) | copy-start | bytes 6148
  97.3 12.0 %copy-start.53 = (f32[512]{0:T(512)}, f32[512]{0:T(512)S(1)}, u32[]{:S(2)}) copy-start(f32[512]{0:T(512)S(1)} %fusion.100) | copy-start | bytes 6148
  97.3 31.0 %all-to-all-start.4 = ((bf16[224,4,896]{2,0,1:T(8,128)(2,1)}), bf16[224,4,896]{2,0,1:T(8,128)(2,1)}, u32[]{:S(2)}, u32[]{:S(2)}) async-start(bf16[224,4,896]{2,0,1:T(8,128)(2,1)} %copy.138), calls=%async_computation.4 | async-start | bytes 3211264 | tf_op jit(solution)/shard_map/all_to_all | solution.py:600
  101.7 342.7 %reduce-scatter.2.cloned.1.call-start = ((), (), s32[]{:S(2)}) async-start(), calls=%async_computation.8 | async-start | bytes 8028160 | tf_op jit(solution)/shard_map/reduce_scatter | solution.py:790
  116.3 15.2 %copy-start.1 = (f32[1,896,896]{2,1,0:T(8,128)S(1)}, f32[1,896,896]{2,1,0:T(8,128)}, u32[]{:S(2)}) copy-start(f32[1,896,896]{2,1,0:T(8,128)} %param.40) | copy-start | bytes 9633796
  118.4 14.6 %copy-start.72 = (f32[64]{0:T(128)}, f32[64]{0:T(128)S(1)}, u32[]{:S(2)}) copy-start(f32[64]{0:T(128)S(1)} %get-tuple-element.403) | copy-start | bytes 772
  118.4 14.6 %copy-start.61 = (f32[64]{0:T(128)}, f32[64]{0:T(128)S(1)}, u32[]{:S(2)}) copy-start(f32[64]{0:T(128)S(1)} %fusion.103) | copy-start | bytes 772
  299.2 13.3 %copy-start.43 = (f32[896]{0:T(1024)S(1)}, f32[896]{0:T(1024)}, u32[]{:S(2)}) copy-start(f32[896]{0:T(1024)} %copy-done.42) | copy-start | bytes 10756
  299.2 13.3 %copy-start.62 = (f32[64]{0:T(128)S(1)}, f32[64]{0:T(128)}, u32[]{:S(2)}) copy-start(f32[64]{0:T(128)} %copy-done.61) | copy-start | bytes 772
  299.2 13.4 %copy-start.73 = (f32[64]{0:T(128)S(1)}, f32[64]{0:T(128)}, u32[]{:S(2)}) copy-start(f32[64]{0:T(128)} %copy-done.72) | copy-start | bytes 772
  299.2 13.5 %copy-start.23 = (bf16[64,896]{1,0:T(8,128)(2,1)S(1)}, bf16[64,896]{1,0:T(8,128)(2,1)}, u32[]{:S(2)}) copy-start(bf16[64,896]{1,0:T(8,128)(2,1)} %fusion.89.refs_0_) | copy-start | bytes 344068
  299.2 13.6 %copy-start.29 = (bf16[64,896]{1,0:T(8,128)(2,1)S(1)}, bf16[64,896]{1,0:T(8,128)(2,1)}, u32[]{:S(2)}) copy-start(bf16[64,896]{1,0:T(8,128)(2,1)} %get-tuple-element.264) | copy-start | bytes 344068
  316.1 12.6 %copy-start.8 = (bf16[512,896]{1,0:T(8,128)(2,1)S(1)}, bf16[512,896]{1,0:T(8,128)(2,1)}, u32[]{:S(2)}) copy-start(bf16[512,896]{1,0:T(8,128)(2,1)} %copy-done.7) | copy-start | bytes 2752516
  316.1 12.6 %copy-start.52 = (f32[896]{0:T(1024)S(1)}, f32[896]{0:T(1024)}, u32[]{:S(2)}) copy-start(f32[896]{0:T(1024)} %copy-done.51) | copy-start | bytes 10756
  316.1 12.7 %copy-start.54 = (f32[512]{0:T(512)S(1)}, f32[512]{0:T(512)}, u32[]{:S(2)}) copy-start(f32[512]{0:T(512)} %copy-done.53) | copy-start | bytes 6148
  342.1 7.7 %copy-start.49 = (f32[512]{0:T(512)S(1)}, f32[512]{0:T(512)}, u32[]{:S(2)}) copy-start(f32[512]{0:T(512)} %copy-done.48) | copy-start | bytes 6148
  351.6 34.7 %copy-start.9 = (bf16[4,64,896]{2,1,0:T(8,128)(2,1)S(1)}, bf16[4,64,896]{2,1,0:T(8,128)(2,1)}, u32[]{:S(2)}) copy-start(bf16[4,64,896]{2,1,0:T(8,128)(2,1)} %exchange_3.1) | copy-start | bytes 1376260
  351.6 34.7 %copy-start.27 = (bf16[256,896]{1,0:T(8,128)(2,1)S(1)}, bf16[256,896]{1,0:T(8,128)(2,1)}, u32[]{:S(2)}) copy-start(bf16[256,896]{1,0:T(8,128)(2,1)} %copy-done.26) | copy-start | bytes 1376260
  353.7 34.4 %copy-start.46 = (s32[2048]{0:T(1024)S(1)}, s32[2048]{0:T(1024)}, u32[]{:S(2)}) copy-start(s32[2048]{0:T(1024)} %sub.146) | copy-start | bytes 24580
  353.7 34.4 %copy-start.55 = (f32[2048]{0:T(1024)S(1)}, f32[2048]{0:T(1024)}, u32[]{:S(2)}) copy-start(f32[2048]{0:T(1024)} %convert_element_type.201) | copy-start | bytes 24580
  353.7 34.4 %copy-start.56 = (f32[2048]{0:T(1024)S(1)}, f32[2048]{0:T(1024)}, u32[]{:S(2)}) copy-start(f32[2048]{0:T(1024)} %sub.151) | copy-start | bytes 24580
  388.1 8.5 %copy-start.21 = (bf16[32,24,896]{2,1,0:T(8,128)(2,1)S(1)}, bf16[32,24,896]{2,1,0:T(8,128)(2,1)}, u32[]{:S(2)}) copy-start(bf16[32,24,896]{2,1,0:T(8,128)(2,1)} %exchange_9.1) | copy-start | bytes 4128772
  388.1 8.5 %copy-start.68 = (s32[768]{0:T(1024)S(1)}, s32[768]{0:T(1024)}, u32[]{:S(2)}) copy-start(s32[768]{0:T(1024)} %copy-done.67) | copy-start | bytes 9220
  396.7 3.8 copy-start.31
  396.7 3.8 copy-start.33
  396.7 3.8 copy-start.35
  396.7 3.8 copy-start.39
  396.7 3.8 copy-start.41
  401.2 4.0 copy-start.50
  401.2 32.2 %copy-start.44 = (f32[32,64]{1,0:T(8,128)S(1)}, f32[32,64]{1,0:T(8,128)}, u32[]{:S(2)}) copy-start(f32[32,64]{1,0:T(8,128)} %get-tuple-element.320) | copy-start | bytes 24580
  401.2 32.4 %copy-start.37 = (s32[8,64,8]{1,2,0:T(8,128)S(1)}, s32[8,64,8]{1,2,0:T(8,128)}, u32[]{:S(2)}) copy-start(s32[8,64,8]{1,2,0:T(8,128)} %copy-done.36) | copy-start | bytes 49156
  401.2 38.6 %copy-start.11 = (f32[256,896]{1,0:T(8,128)S(1)}, f32[256,896]{1,0:T(8,128)}, u32[]{:S(2)}) copy-start(f32[256,896]{1,0:T(8,128)} %copy-done.10) | copy-start | bytes 2752516
  401.2 38.6 %copy-start.28 = (bf16[4,64,896]{2,1,0:T(8,128)(2,1)S(1)}, bf16[4,64,896]{2,1,0:T(8,128)(2,1)}, u32[]{:S(2)}) copy-start(bf16[4,64,896]{2,1,0:T(8,128)(2,1)} %exchange_7.1) | copy-start | bytes 1376260
  401.2 41.7 %all-to-all-start.5 = ((bf16[4,224,896]{2,1,0:T(8,128)(2,1)}), bf16[4,224,896]{2,1,0:T(8,128)(2,1)S(1)}, u32[]{:S(2)}, u32[]{:S(2)}) async-start(bf16[4,224,896]{2,1,0:T(8,128)(2,1)} %bitcast.30), calls=%async_computation.6 | async-start | bytes 3211264 | tf_op jit(solution)/shard_map/all_to_all | solution.py:761
  481.0 8.9 %copy-start.16 = (f32[1,224,896]{2,1,0:T(8,128)S(1)}, f32[1,224,896]{2,1,0:T(8,128)}, u32[]{:S(2)}) copy-start(f32[1,224,896]{2,1,0:T(8,128)} %param.38) | copy-start | bytes 2408452
  481.0 8.9 %copy-start.24 = (f32[1,224,896]{2,1,0:T(8,128)S(1)}, f32[1,224,896]{2,1,0:T(8,128)}, u32[]{:S(2)}) copy-start(f32[1,224,896]{2,1,0:T(8,128)} %param.45) | copy-start | bytes 2408452
  481.0 8.9 %copy-start.25 = (f32[1,224,896]{2,1,0:T(8,128)S(1)}, f32[1,224,896]{2,1,0:T(8,128)}, u32[]{:S(2)}) copy-start(f32[1,224,896]{2,1,0:T(8,128)} %param.52) | copy-start | bytes 2408452
  493.2 6.5 %copy-start.75 = (f32[112]{0:T(128)S(1)}, f32[112]{0:T(128)}, u32[]{:S(2)}) copy-start(f32[112]{0:T(128)} %param.43) | copy-start | bytes 1348
  493.2 6.5 %copy-start.76 = (f32[112]{0:T(128)S(1)}, f32[112]{0:T(128)}, u32[]{:S(2)}) copy-start(f32[112]{0:T(128)} %param.50) | copy-start | bytes 1348
  493.2 6.5 %copy-start.77 = (f32[112]{0:T(128)S(1)}, f32[112]{0:T(128)}, u32[]{:S(2)}) copy-start(f32[112]{0:T(128)} %param.57) | copy-start | bytes 1348
  493.2 7.2 %copy-start.2 = (f32[1,896,896]{2,1,0:T(8,128)S(1)}, f32[1,896,896]{2,1,0:T(8,128)}, u32[]{:S(2)}) copy-start(f32[1,896,896]{2,1,0:T(8,128)} %param.40) | copy-start | bytes 9633796
  493.2 7.2 %copy-start.12 = (f32[1,896,896]{2,1,0:T(8,128)S(1)}, f32[1,896,896]{2,1,0:T(8,128)}, u32[]{:S(2)}) copy-start(f32[1,896,896]{2,1,0:T(8,128)} %param.47) | copy-start | bytes 9633796
  493.3 7.2 %copy-start.13 = (f32[1,896,896]{2,1,0:T(8,128)S(1)}, f32[1,896,896]{2,1,0:T(8,128)}, u32[]{:S(2)}) copy-start(f32[1,896,896]{2,1,0:T(8,128)} %param.54) | copy-start | bytes 9633796
  493.3 8.1 %copy-start.14 = (f32[896,896]{1,0:T(8,128)S(1)}, f32[896,896]{1,0:T(8,128)}, u32[]{:S(2)}) copy-start(f32[896,896]{1,0:T(8,128)} %get-tuple-element.409) | copy-start | bytes 9633796
  501.3 5.7 %copy-start.4 = (f32[1,224,3584]{2,1,0:T(8,128)S(1)}, f32[1,224,3584]{2,1,0:T(8,128)}, u32[]{:S(2)}) copy-start(f32[1,224,3584]{2,1,0:T(8,128)} %param.39) | copy-start | bytes 9633796
  501.3 5.7 %copy-start.5 = (f32[1,224,3584]{2,1,0:T(8,128)S(1)}, f32[1,224,3584]{2,1,0:T(8,128)}, u32[]{:S(2)}) copy-start(f32[1,224,3584]{2,1,0:T(8,128)} %mul.722) | copy-start | bytes 9633796
  501.3 7.1 %copy-start.17 = (f32[1,224,3584]{2,1,0:T(8,128)S(1)}, f32[1,224,3584]{2,1,0:T(8,128)}, u32[]{:S(2)}) copy-start(f32[1,224,3584]{2,1,0:T(8,128)} %param.46) | copy-start | bytes 9633796
  501.3 8.1 %copy-start.18 = (f32[1,224,3584]{2,1,0:T(8,128)S(1)}, f32[1,224,3584]{2,1,0:T(8,128)}, u32[]{:S(2)}) copy-start(f32[1,224,3584]{2,1,0:T(8,128)} %param.53) | copy-start | bytes 9633796
  509.4 4.6 copy-start.60
  509.4 4.6 copy-start.69
  509.4 4.6 copy-start.70
  (19 other events, 29.1 us)
Sparse Core Ops, SparseCore 0:
  10.7 63.1 all-gather.1
  341.4 80.2 reduce-scatter.1
